TPU v7x, 256 devices: a whole 4x4x8 slice. The times are simulated.
256 devices in a mesh: chain: 128 (over x, z, y), side: 2 (over core).
Axes of the slice: x: 4, y: 4, z: 8, core: 2. Of those that a mesh axis runs over, the one named last changes fastest.
Arguments:
- rhs: float32 [8, 262144], P(None, ('chain', 'side')), may hold values from -0.3 to 0.3
- lower_blocks: bfloat16 [4096, 13, 4096], P(('chain', 'side')), may hold values from -0.03 to 0.03
- lower_cols: int32 [4096, 13], P(('chain', 'side')), may hold values from -1 to 14, as said below
- upper_blocks: bfloat16 [4096, 13, 4096], P(('chain', 'side')), may hold values from -0.03 to 0.03
- upper_cols: int32 [4096, 13], P(('chain', 'side')), may hold values from -1 to 15, as said below
- diag_inverse: bfloat16 [4096, 4096], P(('chain', 'side')), may hold values from -0.375 to 1.25, as said below
- link_lower: bfloat16 [4096, 4096], P(('chain', 'side')), may hold values from -1 to 1
- link_upper: bfloat16 [4096, 4096], P(('chain', 'side')), may hold values from -4 to 4
- row_counts: int32 [256], P(('chain', 'side')), may hold values from 8 to 16, as said below
Outputs:
- solution: float32 [8, 262144], P(None, ('chain', 'side'))
Inputs may be any that keep to these rules, and one draw needn't show every extreme that they name: `lower_cols`: entry e of block row k (k counted within its slab) is -1 or a row of the same slab before k; entry 0 is k - 1, or -1 when k is 0. `upper_cols`: entry e of block row k (k counted within its slab) is -1 or a row of the same slab after k; entry 0 is k + 1, or -1 when k is 15. The first row_counts[d] block rows of slab d are active. `diag_inverse`: block g is the inverse of block row g's pivot.
All inputs are finite; a program needn't handle non-finite values.
Results may differ from a plain program's by a relative error of at most 0.00085.
Values sent between devices are 32-bit elements; how exact they have to be, the bound alone decides.
A program may use at most 64 MiB of HBM per device.

v0:
```python
import jax
import jax.numpy as jnp
from jax import lax
from jax.sharding import PartitionSpec as P

NODE_UNKNOWNS = 64
R = 8


def partner_2(value, axis, stride):
    mask = 2**stride
    pairs = [(source, source ^ mask) for source in range(lax.axis_size(axis))]
    return lax.ppermute(value, axis, pairs)


def carried_in(value, axis, join, neutral, backward):
    count, mine = (lax.axis_size(axis), lax.axis_index(axis))
    pieces = jax.tree.map(lambda part: lax.all_gather(part, axis), value)
    if backward:
        pieces = jax.tree.map(lambda part: part[::-1], pieces)
        mine = count - 1 - mine
    so_far = jax.tree.map(
        lambda part, zero: jnp.full_like(part, 0) + jnp.asarray(zero, part.dtype), value, neutral
    )

    def hop(position, so_far):
        longer = join(so_far, jax.tree.map(lambda part: part[position], pieces))
        return jax.tree.map(lambda new, old: jnp.where(position < mine, new, old), longer, so_far)

    return lax.fori_loop(0, count - 1, hop, so_far)


def times_transposed(left, right):
    return lax.dot_general(
        left,
        right,
        (((1,), (1,)), ((), ())),
        precision=lax.Precision.HIGHEST,
        preferred_element_type=jnp.float32,
    )


def times_plain(left, right):
    return jnp.dot(left, right, precision=lax.Precision.HIGHEST, preferred_element_type=jnp.float32)


def compose(earlier, following):
    return (
        times_plain(earlier[0], following[0]),
        times_plain(earlier[1], following[0]) + following[1],
    )


def as_block(flat):
    return flat.astype(jnp.float32).reshape(NODE_UNKNOWNS, NODE_UNKNOWNS)


def sweep(start_rows, blocks, columns, link, inverse, active_rows, descending):
    total_rows = columns.shape[0]
    listed = columns.shape[1]
    width = start_rows.shape[1]
    column_index = lax.broadcasted_iota(jnp.int32, start_rows.shape, 1)
    masked = jnp.where(column_index < active_rows * NODE_UNKNOWNS, start_rows, 0.0)
    work = jnp.concatenate([masked, jnp.zeros((NODE_UNKNOWNS, width), jnp.float32)], axis=0)
    all_rows = work.shape[0]
    work = jnp.concatenate([work, jnp.zeros((all_rows, NODE_UNKNOWNS), jnp.float32)], axis=1)
    seed_rows = jnp.concatenate(
        [jnp.zeros((R, NODE_UNKNOWNS), jnp.float32), jnp.eye(NODE_UNKNOWNS, dtype=jnp.float32)],
        axis=0,
    )

    def one_row(step, current):
        row_index = total_rows - 1 - step if descending else step
        start_shift = row_index * NODE_UNKNOWNS
        total = lax.dynamic_slice_in_dim(current, start_shift, NODE_UNKNOWNS, 1)
        total = total - times_transposed(seed_rows, as_block(link[row_index]))
        entries = columns[row_index]
        picked = jnp.where(entries >= 0, entries, total_rows)
        listed_tiles = jnp.take(
            current.reshape(all_rows, total_rows + 1, NODE_UNKNOWNS), picked, axis=1
        )
        factors = (
            blocks[row_index].astype(jnp.float32).reshape(listed, NODE_UNKNOWNS, NODE_UNKNOWNS)
        )
        total = total - lax.dot_general(
            listed_tiles,
            factors,
            (((1, 2), (0, 2)), ((), ())),
            precision=lax.Precision.HIGHEST,
            preferred_element_type=jnp.float32,
        )
        if inverse is not None:
            total = times_transposed(total, as_block(inverse[row_index]))
        total = jnp.where(row_index < active_rows, total, 0.0)
        return lax.dynamic_update_slice_in_dim(current, total, start_shift, 1)

    finished = lax.fori_loop(0, total_rows, one_row, work)
    return finished[:, :width]


def local(
    rhs,
    lower_blocks,
    lower_cols,
    upper_blocks,
    upper_cols,
    diag_inverse,
    link_lower,
    link_upper,
    row_counts,
):
    active_rows = row_counts[0]
    identity_map = (
        jnp.eye(NODE_UNKNOWNS, dtype=jnp.float32),
        jnp.zeros((R, NODE_UNKNOWNS), jnp.float32),
    )
    forward_workload = sweep(rhs, lower_blocks, lower_cols, link_lower, None, active_rows, False)
    boundary = lax.dynamic_slice_in_dim(
        forward_workload, (active_rows - 1) * NODE_UNKNOWNS, NODE_UNKNOWNS, 1
    )
    own_map = (boundary[R:], boundary[:R])
    partner = partner_2((own_map[0], own_map[1]), "side", 0)
    leading = lax.axis_index("side") == 0
    earlier_map = (
        jnp.where(leading, own_map[0], partner[0]),
        jnp.where(leading, own_map[1], partner[1]),
    )
    following_map = (
        jnp.where(leading, partner[0], own_map[0]),
        jnp.where(leading, partner[1], own_map[1]),
    )
    before = carried_in(compose(earlier_map, following_map), "chain", compose, identity_map, False)
    incoming = jnp.where(leading, before[1], times_plain(before[1], partner[0]) + partner[1])
    forward_direction = forward_workload[:R] + times_plain(incoming, forward_workload[R:])
    backward_work = sweep(
        forward_direction, upper_blocks, upper_cols, link_upper, diag_inverse, active_rows, True
    )
    boundary = backward_work[:, :NODE_UNKNOWNS]
    own_map = (boundary[R:], boundary[:R])
    partner = partner_2((own_map[0], own_map[1]), "side", 0)
    leading = lax.axis_index("side") == 1
    earlier_map = (
        jnp.where(leading, own_map[0], partner[0]),
        jnp.where(leading, own_map[1], partner[1]),
    )
    following_map = (
        jnp.where(leading, partner[0], own_map[0]),
        jnp.where(leading, partner[1], own_map[1]),
    )
    after = carried_in(compose(earlier_map, following_map), "chain", compose, identity_map, True)
    incoming = jnp.where(leading, after[1], times_plain(after[1], partner[0]) + partner[1])
    return backward_work[:R] + times_plain(incoming, backward_work[R:])


def solution(mesh):
    return jax.shard_map(
        local,
        mesh=mesh,
        in_specs=(
            P(None, ("chain", "side")),
            P(("chain", "side"), None, None),
            P(("chain", "side"), None),
            P(("chain", "side"), None, None),
            P(("chain", "side"), None),
            P(("chain", "side"), None),
            P(("chain", "side"), None),
            P(("chain", "side"), None),
            P(("chain", "side")),
        ),
        out_specs=P(None, ("chain", "side")),
        check_vma=False,
    )
```

profile of v0, /device:TPU:8, one launch (start us, length us, event | category | flops | bytes accessed | tf_op | source)
XLA Modules:
  0.0 1086.0 jit_solution(6205306625136570755)
XLA Ops:
  8.8 2.4 copy.18
  11.2 60.3 %while.56 = (s32[]{:T(128)}, f32[72,1088]{0,1:T(8,128)S(1)}, s32[]{:T(128)}, bf16[16,4096]{1,0:T(8,128)(2,1)}, f32[72,64]{1,0:T(8,128)S(1)}, /*index=5*/s32[16,1...) while((s32[]{:T(128)}, f32[72,1088]{0,1:T(8,128)S(1)}, ...), condition=%wide.region_1.3_spmd, body=%wide.region_0.2_spmd.sunk | while | flops 49620076 | bytes 1458599 | solution.py:97
  72.0 1.2 collective-permute-done
  74.3 2.4 copy.22
  76.9 345.0 %all-gather.1 = f32[1024,64]{1,0:T(8,128)S(1)} all-gather(f32[8,64]{1,0:T(8,128)S(1)} %convolution_add_fusion.5), channel_id=3, replica_groups=mesh['chain'=128,'side'=2] {'chain'}, dimensions={0}, use_global_device_ids=true | all-gather | bytes 264192 | tf_op jit(solution)/shard_map/all_gather | solution.py:18
  421.9 115.8 %while.58 = (s32[]{:T(128)}, f32[8,64]{1,0:T(8,128)S(1)}, s32[]{:T(128)}, f32[128,64,64]{2,1,0:T(8,128)}, f32[128,8,64]{2,1,0:T(8,128)S(1)}, /*index=5*/s32[]{:T(128)}, s32[]{:T(128)}) while((s32[]{:T(128)}, f32[8,64]{1,0:T(8,128)S(1)}, s32[]{:T(128)}, f32[128,64,64]{2,1,0:T(8,128)}, f32[128,8,64]{2,1,0:T(8,128)S(1)}, ...), condition=%wide.region_3.5_spmd.clone, body=%wide.region_2.4_spmd.clone.sunk | while | flops 395268 | bytes 53863 | solution.py:30
  422.8 0.9 fusion.103
  432.8 0.9 fusion.103
  433.7 0.9 fusion.103
  434.7 0.9 fusion.103
  435.6 0.9 fusion.103
  436.5 0.9 fusion.103
  437.4 0.9 fusion.103
  438.3 0.9 fusion.103
  439.2 0.9 fusion.103
  440.1 0.9 fusion.103
  450.2 0.9 fusion.103
  451.1 0.9 fusion.103
  452.0 0.9 fusion.103
  452.9 0.9 fusion.103
  453.8 0.9 fusion.103
  454.7 0.9 fusion.103
  455.6 0.9 fusion.103
  456.5 0.9 fusion.103
  457.4 0.9 fusion.103
  467.5 0.9 fusion.103
  468.4 0.9 fusion.103
  469.3 0.9 fusion.103
  470.2 0.9 fusion.103
  471.1 0.9 fusion.103
  472.0 0.9 fusion.103
  472.9 0.9 fusion.103
  473.9 0.9 fusion.103
  474.8 0.9 fusion.103
  484.8 0.9 fusion.103
  485.7 0.9 fusion.103
  486.6 0.9 fusion.103
  487.5 0.9 fusion.103
  488.4 0.9 fusion.103
  538.6 1.3 fusion.37
  540.2 65.4 %while.57 = (s32[]{:T(128)}, f32[72,1088]{0,1:T(8,128)S(1)}, s32[]{:T(128)}, bf16[16,4096]{1,0:T(8,128)(2,1)}, f32[72,64]{1,0:T(8,128)S(1)}, /*index=5*/s32[16,1...) while((s32[]{:T(128)}, f32[72,1088]{0,1:T(8,128)S(1)}, ...), condition=%wide.region_5.7_spmd, body=%wide.region_4.6_spmd.sunk | while | flops 53159024 | bytes 1503729 | solution.py:97
  541.6 1.0 dynamic-slice_reduce_fusion.6
  545.7 1.0 dynamic-slice_reduce_fusion.6
  549.7 1.0 dynamic-slice_reduce_fusion.6
  553.8 1.0 dynamic-slice_reduce_fusion.6
  557.9 1.0 dynamic-slice_reduce_fusion.6
  562.0 1.0 dynamic-slice_reduce_fusion.6
  566.1 1.0 dynamic-slice_reduce_fusion.6
  570.2 1.0 dynamic-slice_reduce_fusion.6
  574.3 1.0 dynamic-slice_reduce_fusion.6
  578.4 1.0 dynamic-slice_reduce_fusion.6
  582.5 1.0 dynamic-slice_reduce_fusion.6
  586.6 1.0 dynamic-slice_reduce_fusion.6
  590.6 1.0 dynamic-slice_reduce_fusion.6
  594.7 1.0 dynamic-slice_reduce_fusion.6
  598.8 1.0 dynamic-slice_reduce_fusion.6
  602.9 1.0 dynamic-slice_reduce_fusion.6
  605.7 1.2 collective-permute-done.2
  606.9 0.9 fusion.42
  608.4 1.0 collective-permute-done.3
  609.6 347.6 %all-gather.3 = f32[1024,64]{1,0:T(8,128)S(1)} all-gather(f32[8,64]{1,0:T(8,128)S(1)} %convolution_add_fusion.3), channel_id=5, replica_groups=mesh['chain'=128,'side'=2] {'chain'}, dimensions={0}, use_global_device_ids=true | all-gather | bytes 264192 | tf_op jit(solution)/shard_map/all_gather | solution.py:18
  957.2 4.7 rev.6
  962.0 115.8 %while.59 = (s32[]{:T(128)}, f32[8,64]{1,0:T(8,128)S(1)}, s32[]{:T(128)}, f32[128,64,64]{2,1,0:T(8,128)}, f32[128,8,64]{2,1,0:T(8,128)S(1)}, /*index=5*/s32[]{:T(128)}, s32[]{:T(128)}) while((s32[]{:T(128)}, f32[8,64]{1,0:T(8,128)S(1)}, s32[]{:T(128)}, f32[128,64,64]{2,1,0:T(8,128)}, f32[128,8,64]{2,1,0:T(8,128)S(1)}, ...), condition=%wide.region_7.9_spmd.clone, body=%wide.region_6.8_spmd.clone.sunk | while | flops 395268 | bytes 53863 | solution.py:30
  1077.9 1.3 convolution_add_fusion
  (817 shorter events, 293.9 us)
Async XLA Ops:
  6.5 415.4 %all-gather.7.cloned.1.call-start = ((), (), s32[]{:S(2)}) async-start(), calls=%async_computation | async-start | bytes 4227072 | tf_op jit(solution)/shard_map/all_gather | solution.py:18
  7.2 0.6 copy-start.1
  71.9 1.3 collective-permute-start
  73.2 3.6 copy-start
  74.0 883.3 %all-gather.9.cloned.1.call-start = ((), (), s32[]{:S(2)}) async-start(), calls=%async_computation.1 | async-start | bytes 4227072 | tf_op jit(solution)/shard_map/all_gather | solution.py:18
  74.1 2.6 collective-permute-start.1
  605.7 1.2 collective-permute-start.2
  608.1 1.3 collective-permute-start.3
Sparse Core Ops, SparseCore 0:
  74.1 119.9 all-gather.6
  608.0 114.1 all-gather.8
where the time goes:
time: 1110 us; the launch traced here: 1090 us
  blocking collectives  693 us (62%)
  matrix products  257 us (23%)
  local copies, waits for them, and re-layouts  71.9 us (6%)
  other arithmetic  23.5 us (2%)
  loops' own time  23.1 us (2%)
  between operations  14.2 us (1%)
    all_gather x2, blocking collectives, carried_in(): pieces = jax.tree.map(lambda part: lax.all_gather(part, axis), value)  693 us
    dot_general x262, matrix products, times_plain(): jnp.dot(left, right, precision=lax.Precision.HIGHEST, preferred_element_t...  236 us
    another operation x2, loops' own time, sweep(): finished = lax.fori_loop(0, total_rows, one_row, work)  22.8 us
    and x32, other arithmetic, one_row(): jnp.take(current.reshape(all_rows, total_rows + 1, NODE_UNKNOWNS), picked...  22.5 us
  transfers between devices with their start and end apart: 6, of which 3 were waited for; matrix products, arithmetic and copies ran while one was open for 0% of the time, Pallas kernels for 0%

commit v1 on v0

v1 whole, which is shorter than its diff:
```python
import functools

import jax
import jax.numpy as jnp
from jax import lax
from jax.experimental import pallas as pl
from jax.experimental.pallas import tpu as pltpu
from jax.sharding import PartitionSpec as P

U = 64
R = 8
NB = 16
KL = 13
F32 = jnp.float32
BF16 = jnp.bfloat16
MESH = pl.DeviceIdType.MESH
NT = (((1,), (1,)), ((), ()))
NN = (((1,), (0,)), ((), ()))
LEVELS = (4, 8, 4)


def split(x):
    hi = x.astype(BF16)
    return hi, (x - hi.astype(F32)).astype(BF16)


def mm(a, b, dims):
    return lax.dot_general(a, b, dims, preferred_element_type=F32)


def dot3(x, w, dims=NN):
    m = x.shape[0]
    xh, xl = split(x)
    wh, wl = split(w)
    both = mm(jnp.concatenate([xh, xl], axis=0), wh, dims)
    return both[:m] + both[m:] + mm(xh, wl, dims)


def dot2(x, w, dims=NN):
    m = x.shape[0]
    xh, xl = split(x)
    both = mm(jnp.concatenate([xh, xl], axis=0), w, dims)
    return both[:m] + both[m:]


def iota(shape, axis):
    return lax.broadcasted_iota(jnp.int32, shape, axis)


def swap_halves(x):
    return pltpu.roll(x, U, axis=1)


def one_hot(cols_ref, active):
    spread = (iota((KL, 256), 1) % 16 == iota((KL, 256), 0)).astype(BF16)
    cols = cols_ref[...].astype(F32).astype(BF16)
    by_row = mm(cols, spread, NN)
    rows = (iota((256, NB), 0) % 16 == iota((256, NB), 1)).astype(BF16)
    listed = mm(rows, by_row.astype(BF16), NN)
    r = iota((256, 256), 0)
    lane = iota((256, 256), 1)
    column = (2 * ((r // 16) % 8) + r // 128).astype(F32)
    keep = (listed == column) & (lane // 16 == r % 16) & (lane % 16 < KL) & (r % 16 < active)
    return jnp.where(keep, 1.0, 0.0).astype(BF16)


def assemble(blocks_ref, cols_ref, active, padded, panel):
    hot = one_hot(cols_ref, active)
    for k in range(NB):
        rows = blocks_ref[k].astype(F32)
        rows = jnp.concatenate([rows, jnp.zeros((16 - KL, U * U), F32)], axis=0)
        padded[pl.ds(16 * k, 16), :] = rows.astype(BF16)
    low = iota((128, 128), 1) < U
    for t in range(16):
        tile = mm(hot, padded[:, pl.ds(256 * t, 256)], NN)
        for s in range(2):
            even = tile[0:128, 128 * s : 128 * s + 128]
            odd = tile[128:256, 128 * s : 128 * s + 128]
            i = 4 * t + 2 * s
            panel[pl.ds(i, 128, stride=U), :] = jnp.where(low, even, swap_halves(odd))
            panel[pl.ds(i + 1, 128, stride=U), :] = jnp.where(low, swap_halves(even), odd)


def spread_rows(flat_ref, out):
    for t in range(32):
        tile = flat_ref[:, pl.ds(128 * t, 128)].astype(F32)
        out[pl.ds(2 * t, NB, stride=U), :] = tile
        out[pl.ds(2 * t + 1, NB, stride=U), :] = swap_halves(tile)


def local_kernel(
    rhs, lower, lcols, upper, ucols, diag, llow, lup, counts, maps, zout,
    padded, pan_l, pan_u, work, dinv, links,
):
    active = counts[0]
    assemble(lower, lcols, active, padded, pan_l)
    assemble(upper, ucols, active, padded, pan_u)
    live = (iota((1, NB * U), 1) // U) < active
    eye = (iota((U, U), 0) == iota((U, U), 1)).astype(BF16)
    spread_rows(llow, links)
    seed = mm(eye, links[:, 0:U].astype(BF16), NT)
    work[0:R, :] = jnp.where(live, rhs[...], 0.0)
    work[R : R + U, :] = jnp.where(live, -seed, 0.0)
    spread_rows(lup, links)
    seed = mm(eye, links[:, 0:U].astype(BF16), NT)
    work[R + U : R + 2 * U, :] = jnp.where(live, -seed, 0.0)
    spread_rows(diag, dinv)
    low = iota((1, 128), 1) < U
    n1 = R + U
    last = jnp.zeros((n1, 128), F32)
    for c in range(8):
        base = c * 1024
        w = work[0:n1, pl.ds(128 * c, 128)]
        x = w - dot3(w, pan_l[pl.ds(base + 128 * c, 128), :], NT)
        work[0:n1, pl.ds(128 * c, 128)] = x
        mine = 2 * c + jnp.where(low, 0, 1) == active - 1
        last = last + jnp.where(mine, x, 0.0)
        rest = 1024 - 128 * (c + 1)
        if rest:
            step = dot3(x, pan_l[pl.ds(base + 128 * (c + 1), rest), :], NT)
            work[0:n1, pl.ds(128 * (c + 1), rest)] -= step
    boundary = last + swap_halves(last)
    z0 = None
    for c in reversed(range(8)):
        base = c * 1024
        v = work[:, pl.ds(128 * c, 128)]
        odd = dot2(v[:, U:128], dinv[pl.ds(128 * c + U, U), 0:U].astype(BF16), NT)
        up = pan_u[pl.ds(base + 128 * c, U), U:128]
        even = v[:, 0:U] - dot3(odd, up, NT)
        even = dot2(even, dinv[pl.ds(128 * c, U), 0:U].astype(BF16), NT)
        z = jnp.concatenate([even, odd], axis=1)
        zout[:, pl.ds(128 * c, 128)] = z
        if c:
            step = dot3(z, pan_u[pl.ds(base, 128 * c), :], NT)
            work[:, pl.ds(0, 128 * c)] -= step
        z0 = z
    maps[0:n1, :] = jnp.where(low, boundary, swap_halves(z0[0:n1]))
    half = n1 + U // 2
    maps[n1:half, :] = jnp.where(low, z0[n1:half], swap_halves(z0[half:]))


def unpack(m):
    low = iota((1, 128), 1) < U
    d = m[R + U :]
    return jnp.concatenate(
        [m[: R + U], jnp.where(low, 0.0, swap_halves(d)), jnp.where(low, 0.0, d)], axis=0
    )


def pack(m):
    low = iota((1, 128), 1) < U
    top, bottom = m[R + U : R + U + U // 2], m[R + U + U // 2 :]
    return jnp.concatenate([m[: R + U], jnp.where(low, swap_halves(top), bottom)], axis=0)


def add_offset(t, m):
    return jnp.concatenate([t[:R] + m[:R], t[R:]], axis=0)


def compose(left, right):
    low = iota((1, 128), 1) < U
    n1 = R + U
    t = add_offset(dot3(left[:n1, :U], right[R:n1]), right)
    weights = jnp.concatenate([jnp.zeros((U, 128), F32), left[n1:]], axis=0)
    s = dot3(jnp.concatenate([t, right[n1:]], axis=0), weights)
    return jnp.concatenate([jnp.where(low, t, s[:n1] + left[:n1]), s[n1:]], axis=0)


def tree(nodes):
    layers = [nodes]
    while len(nodes) > 1:
        nodes = [compose(nodes[i], nodes[i + 1]) for i in range(0, len(nodes), 2)]
        layers.append(nodes)
    return layers


def identity_map():
    r = iota((R + 2 * U, 128), 0)
    lane = iota((R + 2 * U, 128), 1)
    one = ((r >= R) & (r < R + U) & (lane == r - R)) | ((r >= R + U) & (lane == r - R - U + U))
    return jnp.where(one, 1.0, 0.0)


def narrow(layers, index, before, after):
    width = 1
    for nodes in layers[:-1]:
        here = index // width
        sibling = nodes[0]
        for j in range(len(nodes)):
            sibling = jnp.where((here ^ 1) == j, nodes[j], sibling)
        right = here % 2 == 1
        c = compose(jnp.where(right, sibling, after), jnp.where(right, before, sibling))
        before, after = jnp.where(right, c, before), jnp.where(right, after, c)
        width *= 2
    return before, after


def scan_kernel(
    levels, maps, z, out, b_core, b_y, b_z, b_x, s_core, r_core, s_y, r_y, s_z, r_z, s_x, r_x
):
    nx, nz, ny = levels
    chain = lax.axis_index("chain")
    side = lax.axis_index("side")
    y = chain % ny
    zz = (chain // ny) % nz
    x = chain // (ny * nz)

    def at_y(k):
        return (chain - y + (y + k) % ny, side)

    def at_z(k):
        return (chain - zz * ny + ((zz + k) % nz) * ny, side)

    def at_x(k):
        return (((x + k) % nx) * (ny * nz) + chain % (ny * nz), side)

    peers = [(chain, 1 - side)]
    peers += [at_y(k) for k in range(1, ny)]
    peers += [at_z(k) for k in range(1, nz)]
    peers += [at_x(k) for k in range(1, nx)]
    barrier = pltpu.get_barrier_semaphore()
    for peer in peers:
        pl.semaphore_signal(barrier, inc=1, device_id=peer, device_id_type=MESH)
    pl.semaphore_wait(barrier, len(peers))

    def share(value, buf, index, count, peer_of, send, recv):
        buf[index] = value
        order = sorted(range(1, count), key=lambda k: min(k, count - k))
        copies = []
        for k in order:
            copy = pltpu.make_async_remote_copy(
                src_ref=buf.at[index],
                dst_ref=buf.at[index],
                send_sem=send.at[k - 1],
                recv_sem=recv.at[k - 1],
                device_id=peer_of(k),
                device_id_type=MESH,
            )
            copy.start()
            copies.append(copy)
        return copies

    def collect(copies, buf, count):
        for copy in copies:
            copy.wait()
        return [unpack(buf[j]) for j in range(count)]

    copies = share(maps[...], b_core, side, 2, lambda k: (chain, 1 - side), s_core, r_core)
    core_layers = tree(collect(copies, b_core, 2))
    copies = share(pack(core_layers[-1][0]), b_y, y, ny, at_y, s_y, r_y)
    y_layers = tree(collect(copies, b_y, ny))
    copies = share(pack(y_layers[-1][0]), b_z, zz, nz, at_z, s_z, r_z)
    z_layers = tree(collect(copies, b_z, nz))
    copies = share(pack(z_layers[-1][0]), b_x, x, nx, at_x, s_x, r_x)
    before = after = identity_map()
    before, after = narrow(core_layers, side, before, after)
    before, after = narrow(y_layers, y, before, after)
    before, after = narrow(z_layers, zz, before, after)
    groups = collect(copies, b_x, nx)

    n1 = R + U
    t = groups[0][:R]
    p = jnp.zeros((R, U), F32)
    ends = [t]
    for j in range(1, nx):
        p = jnp.where(x == j, t[:, :U], p)
        if j < nx - 1 or True:
            t = dot3(t[:, :U], groups[j][R:n1]) + groups[j][:R]
            ends.append(t)
    q_run = ends[nx - 1][:, U:]
    q = jnp.zeros((R, U), F32)
    for j in reversed(range(nx - 1)):
        q = jnp.where(x == j, q_run, q)
        if j:
            q_run = dot3(q_run, groups[j][n1:, U:]) + ends[j][:, U:]
    own = unpack(maps[...])
    t = dot3(p, before[R:n1, :U]) + before[:R, :U]
    p = t
    t = dot3(p, own[R:n1, :U]) + own[:R, :U]
    t = dot3(t, after[R:n1]) + after[:R]
    q = t[:, U:] + dot3(q, after[n1:, U:])
    pq = jnp.concatenate([p, q], axis=1)
    out[...] = z[0:R, :] + dot3(pq, z[R:, :])


def local(levels, interpret, rhs, lower, lcols, upper, ucols, diag, llow, lup, counts):
    vmem = pl.BlockSpec(memory_space=pltpu.VMEM)
    rows = R + 2 * U
    packed = R + U + U // 2
    maps, z = pl.pallas_call(
        local_kernel,
        out_shape=(
            jax.ShapeDtypeStruct((packed, 128), F32),
            jax.ShapeDtypeStruct((rows, NB * U), F32),
        ),
        in_specs=[vmem] * 8 + [pl.BlockSpec(memory_space=pltpu.SMEM)],
        out_specs=(vmem, vmem),
        scratch_shapes=[
            pltpu.VMEM((256, 4096), BF16),
            pltpu.VMEM((8192, 128), F32),
            pltpu.VMEM((8192, 128), F32),
            pltpu.VMEM((rows, NB * U), F32),
            pltpu.VMEM((NB * U, 128), F32),
            pltpu.VMEM((NB * U, 128), F32),
        ],
        compiler_params=pltpu.CompilerParams(vmem_limit_bytes=48 * 1024 * 1024),
        interpret=interpret,
        name="local_sweeps",
    )(rhs, lower, lcols, upper, ucols, diag, llow, lup, counts)
    if levels is None:
        return maps, z
    nx, nz, ny = levels
    dma = pltpu.SemaphoreType.DMA
    return pl.pallas_call(
        functools.partial(scan_kernel, levels),
        out_shape=jax.ShapeDtypeStruct((R, NB * U), F32),
        in_specs=[vmem, vmem],
        out_specs=vmem,
        scratch_shapes=[pltpu.VMEM((n, packed, 128), F32) for n in (2, ny, nz, nx)]
        + [dma((n - 1,)) for n in (2, 2, ny, ny, nz, nz, nx, nx)],
        compiler_params=pltpu.CompilerParams(
            collective_id=0, has_side_effects=True, vmem_limit_bytes=48 * 1024 * 1024
        ),
        name="slab_scan",
    )(maps, z)


def solution(mesh, levels=LEVELS):
    both = ("chain", "side")
    return jax.shard_map(
        functools.partial(local, levels, False),
        mesh=mesh,
        in_specs=(
            P(None, both),
            P(both, None, None),
            P(both, None),
            P(both, None, None),
            P(both, None),
            P(both, None),
            P(both, None),
            P(both, None),
            P(both),
        ),
        out_specs=P(None, both),
        check_vma=False,
    )
```

time: 1110 us -> 56 us (0.05)
  the two profiles are of different devices: /device:TPU:8 before, /device:TPU:32 now
where the time goes in v1:
time: 56 us; the launch traced here: 55.9 us
  Pallas kernels  51 us (91%)
  local copies, waits for them, and re-layouts  4.03 us (7%)
  between operations  0.91 us (2%)
    pallas_call x1, Pallas kernels, local(): pl.pallas_call(functools.partial(scan_kernel, levels), out_shape=jax.Shap...  37.4 us
    pallas_call x1, Pallas kernels, local(): pl.pallas_call(local_kernel, out_shape=(jax.ShapeDtypeStruct((packed, 128...  13.6 us
    unnamed x17, local copies, waits for them, and re-layouts  4.03 us

profile of v1, /device:TPU:32, one launch (start us, length us, event | category | flops | bytes accessed | tf_op | source)
XLA Modules:
  0.0 55.9 jit_solution(5681131936620566667)
XLA Ops:
  0.0 0.0 copy-start.6
  0.8 2.4 %copy.10.lower = bf16[16,13,4096]{2,1,0:T(8,128)(2,1)S(1)} copy(bf16[16,13,4096]{2,0,1:T(8,128)(2,1)} %param.10) | data formatting | bytes 3407872 | tf_op args[1]
  3.2 0.0 copy-done.6
  3.2 0.0 copy-start
  3.2 0.0 copy-start.1
  3.2 0.0 copy-start.2
  3.2 0.0 copy-start.3
  3.3 0.0 copy-start.4
  3.3 0.0 copy-start.5
  3.3 1.0 %copy.11.upper = bf16[16,13,4096]{2,1,0:T(8,128)(2,1)S(1)} copy(bf16[16,13,4096]{2,0,1:T(8,128)(2,1)S(1)} %copy-done.6) | data formatting | bytes 3407872 | tf_op args[3]
  4.2 0.0 copy-done
  4.3 0.0 copy-done.1
  4.3 0.0 copy-done.2
  4.3 0.0 copy-done.3
  4.3 0.0 copy-done.4
  4.3 0.0 copy-done.5
  4.3 13.6 %local_sweeps.1 = (f32[104,128]{1,0:T(8,128)S(1)}, f32[136,1024]{1,0:T(8,128)S(1)}) custom-call(f32[8,1024]{1,0:T(8,128)S(1)} %copy-done.3, bf16[16,13,4096]{2,1,0:T(8,128)(2,1)S(1)} %copy.10.lower, s32[16,13]{1,0:T(8,128)S(1)} %copy-done.4, bf16[16,13,4096]{2,1,0:T(8,128)(2,1)S(1)} %copy.11.upper, s32[16,13]{1,0:T(8,128)S(1)} %copy-done.5, ...), custom_call_target="tpu_custom_call" | custom-call | tf_op jit(solution)/shard_map/local_sweeps/pallas_call | solution.py:290
  17.9 37.4 %slab_scan.1 = f32[8,1024]{1,0:T(8,128)S(1)} custom-call(f32[104,128]{1,0:T(8,128)S(1)} %get-tuple-element.7.maps, f32[136,1024]{1,0:T(8,128)S(1)} %get-tuple-element.8.z), custom_call_target="tpu_custom_call" | custom-call | tf_op jit(solution)/shard_map/slab_scan/pallas_call | solution.py:314
  55.3 0.6 %copy.14 = f32[8,1024]{1,0:T(8,128)} copy(f32[8,1024]{1,0:T(8,128)S(1)} %slab_scan.1) | data formatting | bytes 65536
Async XLA Ops:
  0.0 3.2 %copy-start.6 = (bf16[16,13,4096]{2,0,1:T(8,128)(2,1)S(1)}, bf16[16,13,4096]{2,0,1:T(8,128)(2,1)}, u32[]{:S(2)}) copy-start(bf16[16,13,4096]{2,0,1:T(8,128)(2,1)} %param.12) | copy-start | bytes 5111812
  3.2 1.0 %copy-start = (bf16[16,4096]{1,0:T(8,128)(2,1)S(1)}, bf16[16,4096]{1,0:T(8,128)(2,1)}, u32[]{:S(2)}) copy-start(bf16[16,4096]{1,0:T(8,128)(2,1)} %diag.1) | copy-start | bytes 393220
  3.2 1.0 %copy-start.1 = (bf16[16,4096]{1,0:T(8,128)(2,1)S(1)}, bf16[16,4096]{1,0:T(8,128)(2,1)}, u32[]{:S(2)}) copy-start(bf16[16,4096]{1,0:T(8,128)(2,1)} %llow.1) | copy-start | bytes 393220
  3.2 1.0 %copy-start.2 = (bf16[16,4096]{1,0:T(8,128)(2,1)S(1)}, bf16[16,4096]{1,0:T(8,128)(2,1)}, u32[]{:S(2)}) copy-start(bf16[16,4096]{1,0:T(8,128)(2,1)} %lup.1) | copy-start | bytes 393220
  3.2 1.0 %copy-start.3 = (f32[8,1024]{1,0:T(8,128)S(1)}, f32[8,1024]{1,0:T(8,128)}, u32[]{:S(2)}) copy-start(f32[8,1024]{1,0:T(8,128)} %rhs.1) | copy-start | bytes 98308
  3.3 1.0 %copy-start.4 = (s32[16,13]{1,0:T(8,128)S(1)}, s32[16,13]{1,0:T(8,128)}, u32[]{:S(2)}) copy-start(s32[16,13]{1,0:T(8,128)} %lcols.1) | copy-start | bytes 2500
  3.3 1.0 %copy-start.5 = (s32[16,13]{1,0:T(8,128)S(1)}, s32[16,13]{1,0:T(8,128)}, u32[]{:S(2)}) copy-start(s32[16,13]{1,0:T(8,128)} %ucols.1) | copy-start | bytes 2500

commit v2 on v1

v2 whole, which is shorter than its diff:
```python
import functools

import jax
import jax.numpy as jnp
from jax import lax
from jax.experimental import pallas as pl
from jax.experimental.pallas import tpu as pltpu
from jax.sharding import PartitionSpec as P

U = 64
R = 8
NB = 16
KL = 13
N1 = R + U
N2 = R + 2 * U
PACKED = R + U + U // 2
PITCH = 72
F32 = jnp.float32
BF16 = jnp.bfloat16
MESH = pl.DeviceIdType.MESH
NT = (((1,), (1,)), ((), ()))
NN = (((1,), (0,)), ((), ()))
LEVELS = (4, 8, 4)
CHUNKS = 4
ROWS = (0, 208, 416, 432, 448, 464)


def split(x):
    hi = x.astype(BF16)
    return hi, (x - hi.astype(F32)).astype(BF16)


def mm(a, b, dims):
    return lax.dot_general(a, b, dims, preferred_element_type=F32)


def dot3(x, w, dims=NN):
    m = x.shape[0]
    xh, xl = split(x)
    wh, wl = split(w)
    both = mm(jnp.concatenate([xh, xl], axis=0), wh, dims)
    return both[:m] + both[m:] + mm(xh, wl, dims)


def iota(shape, axis):
    return lax.broadcasted_iota(jnp.int32, shape, axis)


def lower_half():
    return iota((1, 128), 1) < U


def swap_halves(x):
    return pltpu.roll(x, U, axis=1)


def one_hot(lcols, ucols, active):
    e = iota((KL, 512), 0)
    group = iota((KL, 512), 1) // 16
    low = lcols[...].astype(F32).astype(BF16)
    up = ucols[...].astype(F32).astype(BF16)
    listed = mm(low, (group == e).astype(BF16), NN) + mm(up, (group == e + KL).astype(BF16), NN)
    lane = iota((1, 512), 1)
    k = lane % 16
    own = iota((NB, 512), 0) == iota((NB, 512), 1) % 16
    target = jnp.sum(jnp.where(own, listed, 0.0), axis=0, keepdims=True).astype(jnp.int32)
    target = jnp.where(lane >= ROWS[2], k, target)
    target = jnp.where(lane >= ROWS[3], 16, target)
    target = jnp.where(lane >= ROWS[4], 17, target)
    diag = (lane >= ROWS[2]) & (lane < ROWS[3])
    target = jnp.where((lane < ROWS[5]) & (diag | (k < active)), target, -1)
    r = iota((288, 512), 0)
    second = (r >= 144).astype(jnp.int32)
    column = 2 * (r // 16) - 17 * second
    return jnp.where((column == target) & (k == r % 16), 1.0, 0.0).astype(BF16)


def assemble(sources, lcols, ucols, active, stack, panel, sems):
    width = U * U // CHUNKS
    copies = []
    for q in range(CHUNKS):
        lanes = pl.ds(width * q, width)
        row = []
        for n, src in enumerate(sources):
            copy = pltpu.make_async_copy(
                src.at[:, lanes], stack.at[pl.ds(ROWS[n], ROWS[n + 1] - ROWS[n]), lanes], sems.at[n, q]
            )
            copy.start()
            row.append(copy)
        copies.append(row)
    stack[pl.ds(ROWS[5], 512 - ROWS[5]), :] = jnp.zeros((512 - ROWS[5], U * U), BF16)
    hot = one_hot(lcols, ucols, active)
    low = lower_half()
    tiles = 16 // CHUNKS
    for t in range(16):
        if t % tiles == 0:
            for copy in copies[t // tiles]:
                copy.wait()
        tile = mm(hot, stack[:, pl.ds(256 * t, 256)], NN)
        for s in range(2):
            even = tile[0:144, 128 * s : 128 * s + 128]
            odd = tile[144:288, 128 * s : 128 * s + 128]
            i = 4 * t + 2 * s
            panel[pl.ds(i, 144, stride=PITCH), :] = jnp.where(low, even, swap_halves(odd))
            panel[pl.ds(i + 1, 144, stride=PITCH), :] = jnp.where(low, swap_halves(even), odd)


def block(panel, c2, k):
    return panel[pl.ds((c2 * 16 + k) * PITCH, U), :]


def column_blocks(panel, c2, first, last):
    return jnp.concatenate([block(panel, c2, k) for k in range(first, last)], axis=0)


def pair_operator(panel, c):
    low = lower_half()
    zeros = jnp.zeros((U, 128), F32)
    even, odd = block(panel, c, 2 * c), block(panel, c, 2 * c + 1)
    right = jnp.where(low, 0.0, odd)
    inner = dot3(jnp.where(low, even, 0.0), jnp.concatenate([jnp.where(low, 0.0, even), zeros], axis=0))
    inner = dot3(inner, jnp.concatenate([zeros, right], axis=0))
    return jnp.concatenate([jnp.where(low, even, -inner), right], axis=0)


def forward(rhs, active, panel, work, gt, hacc, ops):
    live = (iota((1, NB * U), 1) // U) < active
    low = lower_half()
    eye = (iota((128, 128), 0) == iota((128, 128), 1)).astype(BF16)
    seeds = -mm(eye, column_blocks(panel, 8, 0, NB).astype(BF16), NT)
    work[0:R, :] = jnp.where(live, rhs[...], 0.0)
    work[R:, :] = seeds
    for c in range(8):
        ops[pl.ds(128 * c, 128), :] = pair_operator(panel, c)
    hacc[...] = jnp.where(iota((U, NB * U), 0) == iota((U, NB * U), 1), 1.0, 0.0)
    zeros = jnp.zeros((U, 128), F32)
    last = jnp.zeros((N1, 128), F32)
    for c in range(8):
        here = pl.ds(128 * c, 128)
        w = work[0:N1, here]
        inner = jnp.concatenate([zeros, jnp.where(low, block(panel, c, 2 * c + 1), 0.0)], axis=0)
        x = w - dot3(w, inner, NT)
        work[0:N1, here] = x
        g = dot3(hacc[:, here], ops[here, :])
        gt[:, here] = g
        mine = 2 * c + jnp.where(low, 0, 1) == active - 1
        last = last + jnp.where(mine, x, 0.0)
        if c < 7:
            rest = pl.ds(128 * (c + 1), 128 * (7 - c))
            work[0:N1, rest] -= dot3(x, column_blocks(panel, c, 2 * c + 2, NB), NT)
            weights = [column_blocks(panel, d, 2 * c, 2 * c + 2) for d in range(c + 1, 8)]
            hacc[:, rest] -= dot3(g, jnp.concatenate(weights, axis=1))
    boundary = last + swap_halves(last)
    weights = jnp.concatenate([jnp.zeros((U, NB * U), F32), gt[...]], axis=0)
    z0 = dot3(work[...], weights, NT)
    return jnp.concatenate([jnp.where(low, boundary, z0[:N1]), z0[N1:]], axis=0)


def backward_step(c, panel, work, zbuf, ops):
    here = pl.ds(128 * c, 128)
    z = dot3(work[:, here], ops[here, :], NT)
    zbuf[:, here] = z
    if c:
        work[:, pl.ds(0, 128 * c)] -= dot3(z, column_blocks(panel, c, 0, 2 * c), NT)


def unpack(m):
    low = lower_half()
    d = m[N1:]
    return jnp.concatenate(
        [m[:N1], jnp.where(low, 0.0, swap_halves(d)), jnp.where(low, 0.0, d)], axis=0
    )


def pack(m):
    top, bottom = m[N1 : N1 + U // 2], m[N1 + U // 2 :]
    return jnp.concatenate([m[:N1], jnp.where(lower_half(), swap_halves(top), bottom)], axis=0)


def compose(left, right):
    t = dot3(left[:N1, :U], right[R:N1])
    t = jnp.concatenate([t[:R] + right[:R], t[R:]], axis=0)
    weights = jnp.concatenate([jnp.zeros((U, 128), F32), left[N1:]], axis=0)
    s = dot3(jnp.concatenate([t, right[N1:]], axis=0), weights)
    return jnp.concatenate([jnp.where(lower_half(), t, s[:N1] + left[:N1]), s[N1:]], axis=0)


def identity_map():
    r = iota((N2, 128), 0)
    lane = iota((N2, 128), 1)
    one = ((r >= R) & (r < N1) & (lane == r - R)) | ((r >= N1) & (lane == r - N1 + U))
    return jnp.where(one, 1.0, 0.0)


def narrow(right, sibling, before, after):
    c = compose(jnp.where(right, sibling, after), jnp.where(right, before, sibling))
    return jnp.where(right, c, before), jnp.where(right, after, c)


def kernel(
    levels, rhs, lower, upper, diag, llow, lup, lcols, ucols, counts, *rest
):
    if levels is None:
        maps, zout, stack, panel, work, zbuf, gt, hacc, ops, in_sems = rest
        active = counts[0]
        assemble((lower, upper, diag, llow, lup), lcols, ucols, active, stack, panel, in_sems)
        maps[...] = pack(forward(rhs, active, panel, work, gt, hacc, ops))
        for c in reversed(range(8)):
            backward_step(c, panel, work, zout, ops)
        return
    (
        out, stack, panel, work, zbuf, gt, hacc, ops, in_sems,
        b_core, b_y, b_z, b_x, y_pairs, z_pairs, z_quads, sides,
        s_core, r_core, s_y, r_y, s_z, r_z, s_x, r_x,
    ) = rest
    nx, nz, ny = levels
    chain = lax.axis_index("chain")
    side = lax.axis_index("side")
    y = chain % ny
    zz = (chain // ny) % nz
    x = chain // (ny * nz)

    def at_core(k):
        return (chain, 1 - side)

    def at_y(k):
        return (chain - y + (y + k) % ny, side)

    def at_z(k):
        return (chain - zz * ny + ((zz + k) % nz) * ny, side)

    def at_x(k):
        return (((x + k) % nx) * (ny * nz) + chain % (ny * nz), side)

    peers = [at_core(1)]
    peers += [at_y(k) for k in range(1, ny)]
    peers += [at_z(k) for k in range(1, nz)]
    peers += [at_x(k) for k in range(1, nx)]
    barrier = pltpu.get_barrier_semaphore()
    for peer in peers:
        pl.semaphore_signal(barrier, inc=1, device_id=peer, device_id_type=MESH)

    def copies_of(buf, index, count, peer_of, send, recv):
        order = sorted(range(1, count), key=lambda k: min(k, count - k))
        return [
            pltpu.make_async_remote_copy(
                src_ref=buf.at[index],
                dst_ref=buf.at[index],
                send_sem=send.at[k - 1],
                recv_sem=recv.at[k - 1],
                device_id=peer_of(k),
                device_id_type=MESH,
            )
            for k in order
        ]

    def start(copies):
        for copy in copies:
            copy.start()

    def wait(copies):
        for copy in copies:
            copy.wait()

    fence = pl.when(chain >= 0)
    active = counts[0]
    assemble((lower, upper, diag, llow, lup), lcols, ucols, active, stack, panel, in_sems)
    b_core[side] = pack(forward(rhs, active, panel, work, gt, hacc, ops))
    pl.semaphore_wait(barrier, len(peers))

    core = copies_of(b_core, side, 2, at_core, s_core, r_core)
    start(core)
    wait(core)

    @fence
    def _():
        b_y[y] = pack(compose(unpack(b_core[0]), unpack(b_core[1])))

    ys = copies_of(b_y, y, ny, at_y, s_y, r_y)
    start(ys)

    @fence
    def _():
        for c in (7, 6, 5):
            backward_step(c, panel, work, zbuf, ops)

    wait(ys)

    @fence
    def _():
        nodes = [compose(unpack(b_y[i]), unpack(b_y[i + 1])) for i in range(0, ny, 2)]
        for i, node in enumerate(nodes):
            y_pairs[i] = node
        b_z[zz] = pack(compose(*nodes))

    zs = copies_of(b_z, zz, nz, at_z, s_z, r_z)
    start(zs)

    @fence
    def _():
        for c in (4, 3, 2, 1, 0):
            backward_step(c, panel, work, zbuf, ops)

    @fence
    def _():
        before = after = identity_map()
        before, after = narrow(side == 1, unpack(b_core[1 - side]), before, after)
        before, after = narrow(y % 2 == 1, unpack(b_y[y + 1 - 2 * (y % 2)]), before, after)
        before, after = narrow(y // 2 == 1, y_pairs[1 - y // 2], before, after)
        sides[0] = before
        sides[1] = after

    wait(zs)

    @fence
    def _():
        nodes = [compose(unpack(b_z[i]), unpack(b_z[i + 1])) for i in range(0, nz, 2)]
        for i, node in enumerate(nodes):
            z_pairs[i] = node
        nodes = [compose(nodes[i], nodes[i + 1]) for i in range(0, nz // 2, 2)]
        for i, node in enumerate(nodes):
            z_quads[i] = node
        b_x[x] = pack(compose(*nodes))

    xs = copies_of(b_x, x, nx, at_x, s_x, r_x)
    start(xs)

    @fence
    def _():
        before, after = sides[0], sides[1]
        before, after = narrow(zz % 2 == 1, unpack(b_z[zz + 1 - 2 * (zz % 2)]), before, after)
        pair = zz // 2
        before, after = narrow(pair % 2 == 1, z_pairs[pair + 1 - 2 * (pair % 2)], before, after)
        before, after = narrow(zz // 4 == 1, z_quads[1 - zz // 4], before, after)
        sides[0] = before
        sides[1] = after

    wait(xs)

    t = b_x[0, 0:R]
    p = jnp.zeros((R, U), F32)
    ends = [t]
    for j in range(1, nx):
        p = jnp.where(x == j, t[:, :U], p)
        t = dot3(t[:, :U], b_x[j, R:N1]) + b_x[j, 0:R]
        ends.append(t)
    q_run = ends[nx - 1][:, U:]
    q = jnp.zeros((R, U), F32)
    for j in reversed(range(nx - 1)):
        q = jnp.where(x == j, q_run, q)
        if j:
            q_run = dot3(q_run, unpack(b_x[j])[N1:, U:]) + ends[j][:, U:]
    own = unpack(b_core[side])
    before, after = sides[0], sides[1]
    p = dot3(p, before[R:N1, :U]) + before[:R, :U]
    t = dot3(p, own[R:N1, :U]) + own[:R, :U]
    t = dot3(t, after[R:N1]) + after[:R]
    q = t[:, U:] + dot3(q, after[N1:, U:])
    out[...] = zbuf[0:R, :] + dot3(jnp.concatenate([p, q], axis=1), zbuf[R:, :])


def local(levels, interpret, rhs, lower, lcols, upper, ucols, diag, llow, lup, counts):
    vmem = pl.BlockSpec(memory_space=pltpu.VMEM)
    anywhere = pl.BlockSpec(memory_space=pl.ANY)
    dma = pltpu.SemaphoreType.DMA
    flat = NB * KL
    lower = jnp.transpose(lower, (1, 0, 2)).reshape(flat, U * U)
    upper = jnp.transpose(upper, (1, 0, 2)).reshape(flat, U * U)
    cols = NB * U
    scratch = [
        pltpu.VMEM((512, U * U), BF16),
        pltpu.VMEM((144 * PITCH, 128), F32),
        pltpu.VMEM((N2, cols), F32),
        pltpu.VMEM((N2, cols), F32),
        pltpu.VMEM((U, cols), F32),
        pltpu.VMEM((U, cols), F32),
        pltpu.VMEM((cols, 128), F32),
        dma((5, CHUNKS)),
    ]
    if levels is None:
        outs = (jax.ShapeDtypeStruct((PACKED, 128), F32), jax.ShapeDtypeStruct((N2, cols), F32))
        params = pltpu.CompilerParams(vmem_limit_bytes=56 * 1024 * 1024)
    else:
        nx, nz, ny = levels
        outs = jax.ShapeDtypeStruct((R, cols), F32)
        scratch += [pltpu.VMEM((n, PACKED, 128), F32) for n in (2, ny, nz, nx)]
        scratch += [pltpu.VMEM((n, N2, 128), F32) for n in (ny // 2, nz // 2, nz // 4, 2)]
        scratch += [dma((n - 1,)) for n in (2, 2, ny, ny, nz, nz, nx, nx)]
        params = pltpu.CompilerParams(
            collective_id=0, has_side_effects=True, vmem_limit_bytes=56 * 1024 * 1024
        )
    return pl.pallas_call(
        functools.partial(kernel, levels),
        out_shape=outs,
        in_specs=[vmem] + [anywhere] * 5 + [vmem] * 2 + [pl.BlockSpec(memory_space=pltpu.SMEM)],
        out_specs=jax.tree.map(lambda _: vmem, outs),
        scratch_shapes=scratch,
        compiler_params=params,
        interpret=interpret,
        name="ilu_apply",
    )(rhs, lower, upper, diag, llow, lup, lcols, ucols, counts)


def solution(mesh, levels=LEVELS):
    both = ("chain", "side")
    return jax.shard_map(
        functools.partial(local, levels, False),
        mesh=mesh,
        in_specs=(
            P(None, both),
            P(both, None, None),
            P(both, None),
            P(both, None, None),
            P(both, None),
            P(both, None),
            P(both, None),
            P(both, None),
            P(both),
        ),
        out_specs=P(None, both),
        check_vma=False,
    )
```

time: 56 us -> 45.4 us (0.81)
  the two profiles are of different devices: /device:TPU:32 before, /device:TPU:2 now
where the time goes in v2:
time: 45.4 us; the launch traced here: 45.1 us
  Pallas kernels  43.1 us (95%)
  local copies, waits for them, and re-layouts  1.38 us (3%)
  between operations  0.66 us (1%)
    pallas_call x1, Pallas kernels, local(): pl.pallas_call(functools.partial(kernel, levels), out_shape=outs, in_spec...  43.1 us
    unnamed x1, local copies, waits for them, and re-layouts  1.38 us

profile of v2, /device:TPU:2, one launch (start us, length us, event | category | flops | bytes accessed | tf_op | source)
XLA Modules:
  0.0 45.1 jit_solution(10767361976469630280)
XLA Ops:
  0.7 43.1 %ilu_apply.1 = f32[8,1024]{1,0:T(8,128)} custom-call(f32[8,1024]{1,0:T(8,128)} %rhs.1, bf16[208,4096]{1,0:T(8,128)(2,1)} %bitcast.6, bf16[208,4096]{1,0:T(8,128)(2,1)} %bitcast.7, bf16[16,4096]{1,0:T(8,128)(2,1)} %diag.1, bf16[16,4096]{1,0:T(8,128)(2,1)} %llow.1, bf16[16,4096]{1,0:T(8,128)(2,1)} %lup.1, s32[16,13]{1,0:T(8,128)} %lcols.1, s32[16,13]{1,0:T(8,128)} %ucols.1, ...), custom_call_target="tpu_custom_call" | custom-call | tf_op jit(solution)/shard_map/ilu_apply/pallas_call | solution.py:392
  43.8 1.4 %copy.12 = f32[8,1024]{1,0:T(8,128)} copy(f32[8,1024]{1,0:T(8,128)} %ilu_apply.1) | data formatting | bytes 65536

commit v3 on v2

--- a/solution.py
+++ b/solution.py
@@ -15,6 +15,7 @@
 N2 = R + 2 * U
 PACKED = R + U + U // 2
 PITCH = 72
+HALF = 56
 F32 = jnp.float32
 BF16 = jnp.bfloat16
 MESH = pl.DeviceIdType.MESH
@@ -211,7 +212,7 @@
     (
         out, stack, panel, work, zbuf, gt, hacc, ops, in_sems,
         b_core, b_y, b_z, b_x, y_pairs, z_pairs, z_quads, sides,
-        s_core, r_core, s_y, r_y, s_z, r_z, s_x, r_x,
+        s_core, r_core, s_y, r_y, s_z, r_z, s_x, r_x, s_f, r_f,
     ) = rest
     nx, nz, ny = levels
     chain = lax.axis_index("chain")
@@ -240,18 +241,15 @@
     for peer in peers:
         pl.semaphore_signal(barrier, inc=1, device_id=peer, device_id_type=MESH)
 
+    def remote(src, dst, send, recv, peer):
+        return pltpu.make_async_remote_copy(
+            src_ref=src, dst_ref=dst, send_sem=send, recv_sem=recv, device_id=peer, device_id_type=MESH
+        )
+
     def copies_of(buf, index, count, peer_of, send, recv):
         order = sorted(range(1, count), key=lambda k: min(k, count - k))
         return [
-            pltpu.make_async_remote_copy(
-                src_ref=buf.at[index],
-                dst_ref=buf.at[index],
-                send_sem=send.at[k - 1],
-                recv_sem=recv.at[k - 1],
-                device_id=peer_of(k),
-                device_id_type=MESH,
-            )
-            for k in order
+            remote(buf.at[index], buf.at[index], send.at[k - 1], recv.at[k - 1], peer_of(k)) for k in order
         ]
 
     def start(copies):
@@ -291,9 +289,17 @@
         nodes = [compose(unpack(b_y[i]), unpack(b_y[i + 1])) for i in range(0, ny, 2)]
         for i, node in enumerate(nodes):
             y_pairs[i] = node
-        b_z[zz] = pack(compose(*nodes))
-
-    zs = copies_of(b_z, zz, nz, at_z, s_z, r_z)
+        b_z[zz, 0:PACKED] = pack(compose(*nodes))
+        b_z[zz, PACKED:] = jnp.zeros((2 * HALF - PACKED, 128), F32)
+
+    mine = pl.ds(pl.multiple_of(side * HALF, 8), HALF)
+    order = sorted(range(1, nz), key=lambda k: min(k, nz - k))
+    zs, forwards = [], []
+    for k in order:
+        part = b_z.at[zz, mine]
+        zs.append(remote(part, part, s_z.at[k - 1], r_z.at[k - 1], at_z(k)))
+        part = b_z.at[(zz + nz - k) % nz, mine]
+        forwards.append(remote(part, part, s_f.at[k - 1], r_f.at[k - 1], at_core(1)))
     start(zs)
 
     @fence
@@ -310,11 +316,16 @@
         sides[0] = before
         sides[1] = after
 
-    wait(zs)
-
-    @fence
-    def _():
-        nodes = [compose(unpack(b_z[i]), unpack(b_z[i + 1])) for i in range(0, nz, 2)]
+    for arriving, forward_copy in zip(zs, forwards):
+        arriving.wait_recv()
+        forward_copy.start()
+    for arriving in zs:
+        arriving.wait_send()
+    wait(forwards)
+
+    @fence
+    def _():
+        nodes = [compose(unpack(b_z[i, 0:PACKED]), unpack(b_z[i + 1, 0:PACKED])) for i in range(0, nz, 2)]
         for i, node in enumerate(nodes):
             z_pairs[i] = node
         nodes = [compose(nodes[i], nodes[i + 1]) for i in range(0, nz // 2, 2)]
@@ -328,7 +339,7 @@
     @fence
     def _():
         before, after = sides[0], sides[1]
-        before, after = narrow(zz % 2 == 1, unpack(b_z[zz + 1 - 2 * (zz % 2)]), before, after)
+        before, after = narrow(zz % 2 == 1, unpack(b_z[zz + 1 - 2 * (zz % 2), 0:PACKED]), before, after)
         pair = zz // 2
         before, after = narrow(pair % 2 == 1, z_pairs[pair + 1 - 2 * (pair % 2)], before, after)
         before, after = narrow(zz // 4 == 1, z_quads[1 - zz // 4], before, after)
@@ -379,15 +390,15 @@
     ]
     if levels is None:
         outs = (jax.ShapeDtypeStruct((PACKED, 128), F32), jax.ShapeDtypeStruct((N2, cols), F32))
-        params = pltpu.CompilerParams(vmem_limit_bytes=56 * 1024 * 1024)
+        params = pltpu.CompilerParams(vmem_limit_bytes=56420000)
     else:
         nx, nz, ny = levels
         outs = jax.ShapeDtypeStruct((R, cols), F32)
-        scratch += [pltpu.VMEM((n, PACKED, 128), F32) for n in (2, ny, nz, nx)]
+        scratch += [pltpu.VMEM((n, m, 128), F32) for n, m in ((2, PACKED), (ny, PACKED), (nz, 2 * HALF), (nx, PACKED))]
         scratch += [pltpu.VMEM((n, N2, 128), F32) for n in (ny // 2, nz // 2, nz // 4, 2)]
-        scratch += [dma((n - 1,)) for n in (2, 2, ny, ny, nz, nz, nx, nx)]
+        scratch += [dma((n - 1,)) for n in (2, 2, ny, ny, nz, nz, nx, nx, nz, nz)]
         params = pltpu.CompilerParams(
-            collective_id=0, has_side_effects=True, vmem_limit_bytes=56 * 1024 * 1024
+            collective_id=0, has_side_effects=True, vmem_limit_bytes=56420000
         )
     return pl.pallas_call(
         functools.partial(kernel, levels),

time: 45.4 us -> 44.5 us (0.980)
  the two profiles are of different devices: /device:TPU:2 before, /device:TPU:1 now
where the time goes in v3:
time: 44.5 us; the launch traced here: 44.2 us
  Pallas kernels  40.8 us (92%)
  local copies, waits for them, and re-layouts  2.76 us (6%)
  between operations  0.67 us (2%)
    pallas_call x1, Pallas kernels, local(): pl.pallas_call(functools.partial(kernel, levels), out_shape=outs, in_spec...  40.8 us
    unnamed x7, local copies, waits for them, and re-layouts  2.76 us

profile of v3, /device:TPU:1, one launch (start us, length us, event | category | flops | bytes accessed | tf_op | source)
XLA Modules:
  0.0 44.2 jit_solution(7759675818156668080)
XLA Ops:
  0.7 0.0 copy-start
  0.7 0.7 %copy-done = f32[8,1024]{1,0:T(8,128)S(1)} copy-done((f32[8,1024]{1,0:T(8,128)S(1)}, f32[8,1024]{1,0:T(8,128)}, u32[]{:S(2)}) %copy-start) | copy-done | bytes 32792
  1.4 0.0 copy-start.1
  1.4 0.7 %copy-done.1 = s32[16,13]{1,0:T(8,128)S(1)} copy-done((s32[16,13]{1,0:T(8,128)S(1)}, s32[16,13]{1,0:T(8,128)}, u32[]{:S(2)}) %copy-start.1) | copy-done | bytes 856
  2.1 0.0 copy-start.2
  2.1 0.7 %copy-done.2 = s32[16,13]{1,0:T(8,128)S(1)} copy-done((s32[16,13]{1,0:T(8,128)S(1)}, s32[16,13]{1,0:T(8,128)}, u32[]{:S(2)}) %copy-start.2) | copy-done | bytes 856
  2.8 40.8 %ilu_apply.1 = f32[8,1024]{1,0:T(8,128)S(1)} custom-call(f32[8,1024]{1,0:T(8,128)S(1)} %copy-done, bf16[208,4096]{1,0:T(8,128)(2,1)} %bitcast.6, bf16[208,4096]{1,0:T(8,128)(2,1)} %bitcast.7, bf16[16,4096]{1,0:T(8,128)(2,1)} %diag.1, bf16[16,4096]{1,0:T(8,128)(2,1)} %llow.1, bf16[16,4096]{1,0:T(8,128)(2,1)} %lup.1, s32[16,13]{1,0:T(8,128)S(1)} %copy-done.1, ...), custom_call_target="tpu_custom_call" | custom-call | tf_op jit(solution)/shard_map/ilu_apply/pallas_call | solution.py:403
  43.6 0.6 %copy.12 = f32[8,1024]{1,0:T(8,128)} copy(f32[8,1024]{1,0:T(8,128)S(1)} %ilu_apply.1) | data formatting | bytes 65536
Async XLA Ops:
  0.7 0.8 %copy-start = (f32[8,1024]{1,0:T(8,128)S(1)}, f32[8,1024]{1,0:T(8,128)}, u32[]{:S(2)}) copy-start(f32[8,1024]{1,0:T(8,128)} %rhs.1) | copy-start | bytes 98308
  1.4 0.7 %copy-start.1 = (s32[16,13]{1,0:T(8,128)S(1)}, s32[16,13]{1,0:T(8,128)}, u32[]{:S(2)}) copy-start(s32[16,13]{1,0:T(8,128)} %lcols.1) | copy-start | bytes 2500
  2.1 0.7 %copy-start.2 = (s32[16,13]{1,0:T(8,128)S(1)}, s32[16,13]{1,0:T(8,128)}, u32[]{:S(2)}) copy-start(s32[16,13]{1,0:T(8,128)} %ucols.1) | copy-start | bytes 2500

commit v4 on v3

--- a/solution.py
+++ b/solution.py
@@ -22,8 +22,8 @@
 NT = (((1,), (1,)), ((), ()))
 NN = (((1,), (0,)), ((), ()))
 LEVELS = (4, 8, 4)
-CHUNKS = 4
-ROWS = (0, 208, 416, 432, 448, 464)
+CHUNKS = 2
+GROUPS = 2 * KL + 3
 
 
 def split(x):
@@ -55,55 +55,70 @@
     return pltpu.roll(x, U, axis=1)
 
 
-def one_hot(lcols, ucols, active):
-    e = iota((KL, 512), 0)
-    group = iota((KL, 512), 1) // 16
+def one_hot(lcols, ucols, active, half):
+    e = iota((KL, 256), 0)
+    group = iota((KL, 256), 1) // 8
     low = lcols[...].astype(F32).astype(BF16)
     up = ucols[...].astype(F32).astype(BF16)
     listed = mm(low, (group == e).astype(BF16), NN) + mm(up, (group == e + KL).astype(BF16), NN)
-    lane = iota((1, 512), 1)
-    k = lane % 16
-    own = iota((NB, 512), 0) == iota((NB, 512), 1) % 16
+    lane = iota((1, 256), 1)
+    group = lane // 8
+    k = lane % 8 + 8 * half
+    own = iota((NB, 256), 0) == iota((NB, 256), 1) % 8 + 8 * half
     target = jnp.sum(jnp.where(own, listed, 0.0), axis=0, keepdims=True).astype(jnp.int32)
-    target = jnp.where(lane >= ROWS[2], k, target)
-    target = jnp.where(lane >= ROWS[3], 16, target)
-    target = jnp.where(lane >= ROWS[4], 17, target)
-    diag = (lane >= ROWS[2]) & (lane < ROWS[3])
-    target = jnp.where((lane < ROWS[5]) & (diag | (k < active)), target, -1)
-    r = iota((288, 512), 0)
-    second = (r >= 144).astype(jnp.int32)
-    column = 2 * (r // 16) - 17 * second
-    return jnp.where((column == target) & (k == r % 16), 1.0, 0.0).astype(BF16)
-
-
-def assemble(sources, lcols, ucols, active, stack, panel, sems):
+    target = jnp.where(group == 2 * KL, k, target)
+    target = jnp.where(group == 2 * KL + 1, 16, target)
+    target = jnp.where(group == 2 * KL + 2, 17, target)
+    target = jnp.where((group < GROUPS) & ((group == 2 * KL) | (k < active)), target, -1)
+    r = iota((144, 256), 0)
+    second = (r >= 72).astype(jnp.int32)
+    column = 2 * (r // 8) - 17 * second
+    return jnp.where((column == target) & (lane % 8 == r % 8), 1.0, 0.0).astype(BF16)
+
+
+def assemble(sources, few, lcols, ucols, active, stack, panel, sems):
     width = U * U // CHUNKS
-    copies = []
-    for q in range(CHUNKS):
-        lanes = pl.ds(width * q, width)
-        row = []
-        for n, src in enumerate(sources):
-            copy = pltpu.make_async_copy(
-                src.at[:, lanes], stack.at[pl.ds(ROWS[n], ROWS[n + 1] - ROWS[n]), lanes], sems.at[n, q]
-            )
-            copy.start()
-            row.append(copy)
-        copies.append(row)
-    stack[pl.ds(ROWS[5], 512 - ROWS[5]), :] = jnp.zeros((512 - ROWS[5], U * U), BF16)
-    hot = one_hot(lcols, ucols, active)
+    copies = {}
+    for copy in few:
+        copy.start()
+    for half in range(2):
+        for q in range(CHUNKS):
+            lanes = pl.ds(width * q, width)
+            row, first = [], 0
+            for n, src in enumerate(sources):
+                count = src.shape[0]
+                copy = pltpu.make_async_copy(
+                    src.at[:, pl.ds(8 * half, 8), lanes],
+                    stack.at[half, pl.ds(first, count), :, lanes],
+                    sems.at[n, half * CHUNKS + q],
+                )
+                copy.start()
+                row.append(copy)
+                first += count
+            copies[half, q] = row
+    stack[:, GROUPS:] = jnp.zeros((2, 32 - GROUPS, 8, U * U), BF16)
     low = lower_half()
     tiles = 16 // CHUNKS
-    for t in range(16):
-        if t % tiles == 0:
-            for copy in copies[t // tiles]:
-                copy.wait()
-        tile = mm(hot, stack[:, pl.ds(256 * t, 256)], NN)
-        for s in range(2):
-            even = tile[0:144, 128 * s : 128 * s + 128]
-            odd = tile[144:288, 128 * s : 128 * s + 128]
-            i = 4 * t + 2 * s
-            panel[pl.ds(i, 144, stride=PITCH), :] = jnp.where(low, even, swap_halves(odd))
-            panel[pl.ds(i + 1, 144, stride=PITCH), :] = jnp.where(low, swap_halves(even), odd)
+    for copy in few:
+        copy.wait()
+    for half in range(2):
+        hot = one_hot(lcols, ucols, active, half)
+        for t in range(16):
+            if t % tiles == 0:
+                for copy in copies[half, t // tiles]:
+                    copy.wait()
+            rows = stack[half, :, :, pl.ds(256 * t, 256)].reshape(256, 256)
+            tile = mm(hot, rows, NN)
+            for s in range(2):
+                even = tile[0:72, 128 * s : 128 * s + 128]
+                odd = tile[72:144, 128 * s : 128 * s + 128]
+                i = 4 * t + 2 * s
+                first = jnp.where(low, even, swap_halves(odd))
+                second = jnp.where(low, swap_halves(even), odd)
+                for c2 in range(9):
+                    base = (c2 * 16 + 8 * half) * PITCH + i
+                    panel[pl.ds(base, 8, stride=PITCH), :] = first[8 * c2 : 8 * c2 + 8]
+                    panel[pl.ds(base + 1, 8, stride=PITCH), :] = second[8 * c2 : 8 * c2 + 8]
 
 
 def block(panel, c2, k):
@@ -199,20 +214,24 @@
 
 
 def kernel(
-    levels, rhs, lower, upper, diag, llow, lup, lcols, ucols, counts, *rest
+    levels, rhs_in, lower, upper, diag, llow, lup, lcols_in, ucols_in, counts, *rest
 ):
     if levels is None:
-        maps, zout, stack, panel, work, zbuf, gt, hacc, ops, in_sems = rest
+        maps, zout, stack, panel, work, zbuf, gt, hacc, ops, in_sems, rhs, lcols, ucols, few_sems = rest
+        few = [
+            pltpu.make_async_copy(src, dst, few_sems.at[n])
+            for n, (src, dst) in enumerate(((lcols_in, lcols), (ucols_in, ucols), (rhs_in, rhs)))
+        ]
         active = counts[0]
-        assemble((lower, upper, diag, llow, lup), lcols, ucols, active, stack, panel, in_sems)
+        assemble((lower, upper, diag, llow, lup), few, lcols, ucols, active, stack, panel, in_sems)
         maps[...] = pack(forward(rhs, active, panel, work, gt, hacc, ops))
         for c in reversed(range(8)):
             backward_step(c, panel, work, zout, ops)
         return
     (
-        out, stack, panel, work, zbuf, gt, hacc, ops, in_sems,
+        out, stack, panel, work, zbuf, gt, hacc, ops, in_sems, rhs, lcols, ucols, few_sems,
         b_core, b_y, b_z, b_x, y_pairs, z_pairs, z_quads, sides,
-        s_core, r_core, s_y, r_y, s_z, r_z, s_x, r_x, s_f, r_f,
+        s_core, r_core, s_y, r_y, s_fy, r_fy, s_z, r_z, s_fz, r_fz, s_x, r_x, s_fx, r_fx,
     ) = rest
     nx, nz, ny = levels
     chain = lax.axis_index("chain")
@@ -221,7 +240,7 @@
     zz = (chain // ny) % nz
     x = chain // (ny * nz)
 
-    def at_core(k):
+    def at_core():
         return (chain, 1 - side)
 
     def at_y(k):
@@ -233,7 +252,7 @@
     def at_x(k):
         return (((x + k) % nx) * (ny * nz) + chain % (ny * nz), side)
 
-    peers = [at_core(1)]
+    peers = [at_core()]
     peers += [at_y(k) for k in range(1, ny)]
     peers += [at_z(k) for k in range(1, nz)]
     peers += [at_x(k) for k in range(1, nx)]
@@ -246,61 +265,67 @@
             src_ref=src, dst_ref=dst, send_sem=send, recv_sem=recv, device_id=peer, device_id_type=MESH
         )
 
-    def copies_of(buf, index, count, peer_of, send, recv):
-        order = sorted(range(1, count), key=lambda k: min(k, count - k))
-        return [
-            remote(buf.at[index], buf.at[index], send.at[k - 1], recv.at[k - 1], peer_of(k)) for k in order
-        ]
-
-    def start(copies):
-        for copy in copies:
+    mine = pl.ds(pl.multiple_of(side * HALF, 8), HALF)
+
+    def put(buf, index, m):
+        buf[index, 0:PACKED] = pack(m)
+        buf[index, PACKED:] = jnp.zeros((2 * HALF - PACKED, 128), F32)
+
+    def ring(buf, index, count, peer_of, send, recv, send_on, recv_on):
+        arrivals, handovers = [], []
+        for k in sorted(range(1, count), key=lambda k: min(k, count - k)):
+            part = buf.at[index, mine]
+            arrivals.append(remote(part, part, send.at[k - 1], recv.at[k - 1], peer_of(k)))
+            part = buf.at[(index + count - k) % count, mine]
+            handovers.append(remote(part, part, send_on.at[k - 1], recv_on.at[k - 1], at_core()))
+        for copy in arrivals:
             copy.start()
-
-    def wait(copies):
-        for copy in copies:
-            copy.wait()
+        return arrivals, handovers
+
+    def finish(copies):
+        for arriving, handover in zip(*copies):
+            arriving.wait_recv()
+            handover.start()
+        for arriving in copies[0]:
+            arriving.wait_send()
+        for handover in copies[1]:
+            handover.wait()
 
     fence = pl.when(chain >= 0)
+    few = [
+        pltpu.make_async_copy(src, dst, few_sems.at[n])
+        for n, (src, dst) in enumerate(((lcols_in, lcols), (ucols_in, ucols), (rhs_in, rhs)))
+    ]
     active = counts[0]
-    assemble((lower, upper, diag, llow, lup), lcols, ucols, active, stack, panel, in_sems)
+    assemble((lower, upper, diag, llow, lup), few, lcols, ucols, active, stack, panel, in_sems)
     b_core[side] = pack(forward(rhs, active, panel, work, gt, hacc, ops))
     pl.semaphore_wait(barrier, len(peers))
 
-    core = copies_of(b_core, side, 2, at_core, s_core, r_core)
-    start(core)
-    wait(core)
-
-    @fence
-    def _():
-        b_y[y] = pack(compose(unpack(b_core[0]), unpack(b_core[1])))
-
-    ys = copies_of(b_y, y, ny, at_y, s_y, r_y)
-    start(ys)
+    core = remote(b_core.at[side], b_core.at[side], s_core, r_core, at_core())
+    core.start()
+    core.wait()
+
+    @fence
+    def _():
+        put(b_y, y, compose(unpack(b_core[0]), unpack(b_core[1])))
+
+    ys = ring(b_y, y, ny, at_y, s_y, r_y, s_fy, r_fy)
 
     @fence
     def _():
         for c in (7, 6, 5):
             backward_step(c, panel, work, zbuf, ops)
 
-    wait(ys)
-
-    @fence
-    def _():
-        nodes = [compose(unpack(b_y[i]), unpack(b_y[i + 1])) for i in range(0, ny, 2)]
+    finish(ys)
+
+    @fence
+    def _():
+        nodes = [compose(unpack(b_y[i, 0:PACKED]), unpack(b_y[i + 1, 0:PACKED])) for i in range(0, ny, 2)]
         for i, node in enumerate(nodes):
             y_pairs[i] = node
-        b_z[zz, 0:PACKED] = pack(compose(*nodes))
-        b_z[zz, PACKED:] = jnp.zeros((2 * HALF - PACKED, 128), F32)
-
-    mine = pl.ds(pl.multiple_of(side * HALF, 8), HALF)
-    order = sorted(range(1, nz), key=lambda k: min(k, nz - k))
-    zs, forwards = [], []
-    for k in order:
-        part = b_z.at[zz, mine]
-        zs.append(remote(part, part, s_z.at[k - 1], r_z.at[k - 1], at_z(k)))
-        part = b_z.at[(zz + nz - k) % nz, mine]
-        forwards.append(remote(part, part, s_f.at[k - 1], r_f.at[k - 1], at_core(1)))
-    start(zs)
+        put(b_z, zz, compose(*nodes))
+
+    zs = ring(b_z, zz, nz, at_z, s_z, r_z, s_fz, r_fz)
 
     @fence
     def _():
@@ -311,17 +336,12 @@
     def _():
         before = after = identity_map()
         before, after = narrow(side == 1, unpack(b_core[1 - side]), before, after)
-        before, after = narrow(y % 2 == 1, unpack(b_y[y + 1 - 2 * (y % 2)]), before, after)
+        before, after = narrow(y % 2 == 1, unpack(b_y[y + 1 - 2 * (y % 2), 0:PACKED]), before, after)
         before, after = narrow(y // 2 == 1, y_pairs[1 - y // 2], before, after)
         sides[0] = before
         sides[1] = after
 
-    for arriving, forward_copy in zip(zs, forwards):
-        arriving.wait_recv()
-        forward_copy.start()
-    for arriving in zs:
-        arriving.wait_send()
-    wait(forwards)
+    finish(zs)
 
     @fence
     def _():
@@ -331,10 +351,9 @@
         nodes = [compose(nodes[i], nodes[i + 1]) for i in range(0, nz // 2, 2)]
         for i, node in enumerate(nodes):
             z_quads[i] = node
-        b_x[x] = pack(compose(*nodes))
-
-    xs = copies_of(b_x, x, nx, at_x, s_x, r_x)
-    start(xs)
+        put(b_x, x, compose(*nodes))
+
+    xs = ring(b_x, x, nx, at_x, s_x, r_x, s_fx, r_fx)
 
     @fence
     def _():
@@ -346,7 +365,7 @@
         sides[0] = before
         sides[1] = after
 
-    wait(xs)
+    finish(xs)
 
     t = b_x[0, 0:R]
     p = jnp.zeros((R, U), F32)
@@ -360,7 +379,7 @@
     for j in reversed(range(nx - 1)):
         q = jnp.where(x == j, q_run, q)
         if j:
-            q_run = dot3(q_run, unpack(b_x[j])[N1:, U:]) + ends[j][:, U:]
+            q_run = dot3(q_run, unpack(b_x[j, 0:PACKED])[N1:, U:]) + ends[j][:, U:]
     own = unpack(b_core[side])
     before, after = sides[0], sides[1]
     p = dot3(p, before[R:N1, :U]) + before[:R, :U]
@@ -374,36 +393,43 @@
     vmem = pl.BlockSpec(memory_space=pltpu.VMEM)
     anywhere = pl.BlockSpec(memory_space=pl.ANY)
     dma = pltpu.SemaphoreType.DMA
-    flat = NB * KL
-    lower = jnp.transpose(lower, (1, 0, 2)).reshape(flat, U * U)
-    upper = jnp.transpose(upper, (1, 0, 2)).reshape(flat, U * U)
+    lower = jnp.transpose(lower, (1, 0, 2))
+    upper = jnp.transpose(upper, (1, 0, 2))
+    diag, llow, lup = diag[None], llow[None], lup[None]
     cols = NB * U
+    lcols, ucols, rhs = (pltpu.with_memory_space_constraint(v, pltpu.HBM) for v in (lcols, ucols, rhs))
+    lower, upper, diag, llow, lup = (pltpu.with_memory_space_constraint(v, pltpu.HBM) for v in (lower, upper, diag, llow, lup))
     scratch = [
-        pltpu.VMEM((512, U * U), BF16),
+        pltpu.VMEM((2, 32, 8, U * U), BF16),
         pltpu.VMEM((144 * PITCH, 128), F32),
         pltpu.VMEM((N2, cols), F32),
         pltpu.VMEM((N2, cols), F32),
         pltpu.VMEM((U, cols), F32),
         pltpu.VMEM((U, cols), F32),
         pltpu.VMEM((cols, 128), F32),
-        dma((5, CHUNKS)),
+        dma((5, 2 * CHUNKS)),
+        pltpu.VMEM((R, cols), F32),
+        pltpu.VMEM((NB, KL), jnp.int32),
+        pltpu.VMEM((NB, KL), jnp.int32),
+        dma((3,)),
     ]
     if levels is None:
         outs = (jax.ShapeDtypeStruct((PACKED, 128), F32), jax.ShapeDtypeStruct((N2, cols), F32))
-        params = pltpu.CompilerParams(vmem_limit_bytes=56420000)
+        params = pltpu.CompilerParams(vmem_limit_bytes=48000000)
     else:
         nx, nz, ny = levels
         outs = jax.ShapeDtypeStruct((R, cols), F32)
-        scratch += [pltpu.VMEM((n, m, 128), F32) for n, m in ((2, PACKED), (ny, PACKED), (nz, 2 * HALF), (nx, PACKED))]
+        scratch += [pltpu.VMEM((2, PACKED, 128), F32)]
+        scratch += [pltpu.VMEM((n, 2 * HALF, 128), F32) for n in (ny, nz, nx)]
         scratch += [pltpu.VMEM((n, N2, 128), F32) for n in (ny // 2, nz // 2, nz // 4, 2)]
-        scratch += [dma((n - 1,)) for n in (2, 2, ny, ny, nz, nz, nx, nx, nz, nz)]
+        scratch += [dma, dma] + [dma((n - 1,)) for n in (ny, nz, nx) for _ in range(4)]
         params = pltpu.CompilerParams(
-            collective_id=0, has_side_effects=True, vmem_limit_bytes=56420000
+            collective_id=0, has_side_effects=True, vmem_limit_bytes=48000000
         )
     return pl.pallas_call(
         functools.partial(kernel, levels),
         out_shape=outs,
-        in_specs=[vmem] + [anywhere] * 5 + [vmem] * 2 + [pl.BlockSpec(memory_space=pltpu.SMEM)],
+        in_specs=[anywhere] * 8 + [pl.BlockSpec(memory_space=pltpu.SMEM)],
         out_specs=jax.tree.map(lambda _: vmem, outs),
         scratch_shapes=scratch,
         compiler_params=params,

time: 44.5 us -> 44 us (0.989)
  local copies, waits for them, and re-layouts: 2.76 us -> 0.62 us
  Pallas kernels: 40.8 us -> 42.7 us
    unnamed x7 -> x1, local copies, waits for them, and re-layouts: 2.76 us -> 0.62 us
    pallas_call x1, Pallas kernels: 40.8 us -> 42.7 us  [local(): pl.pallas_call(functools.partial(kernel, levels), out_shape=outs, in_spec...]
where the time goes in v4:
time: 44 us; the launch traced here: 43.9 us
  Pallas kernels  42.7 us (97%)
  between operations  0.66 us (2%)
  local copies, waits for them, and re-layouts  0.62 us (1%)
    pallas_call x1, Pallas kernels, local(): pl.pallas_call(functools.partial(kernel, levels), out_shape=outs, in_spec...  42.7 us

profile of v4, /device:TPU:1, one launch (start us, length us, event | category | flops | bytes accessed | tf_op | source)
XLA Modules:
  0.0 43.9 jit_solution(12831346128977782134)
XLA Ops:
  0.7 42.7 %ilu_apply.1 = f32[8,1024]{1,0:T(8,128)S(1)} custom-call(f32[8,1024]{1,0:T(8,128)} %rhs_in.1, bf16[13,16,4096]{2,1,0:T(8,128)(2,1)} %bitcast.5, bf16[13,16,4096]{2,1,0:T(8,128)(2,1)} %bitcast.6, bf16[1,16,4096]{2,1,0:T(8,128)(2,1)} %bitcast.7, bf16[1,16,4096]{2,1,0:T(8,128)(2,1)} %bitcast.8, bf16[1,16,4096]{2,1,0:T(8,128)(2,1)} %bitcast.9, ...), custom_call_target="tpu_custom_call" | custom-call | tf_op jit(solution)/shard_map/ilu_apply/pallas_call | solution.py:429
  43.3 0.6 %copy.12 = f32[8,1024]{1,0:T(8,128)} copy(f32[8,1024]{1,0:T(8,128)S(1)} %ilu_apply.1) | data formatting | bytes 65536

commit v5 on v4

--- a/solution.py
+++ b/solution.py
@@ -23,6 +23,7 @@
 NN = (((1,), (0,)), ((), ()))
 LEVELS = (4, 8, 4)
 CHUNKS = 2
+PIECE = 4
 GROUPS = 2 * KL + 3
 
 
@@ -39,8 +40,26 @@
     m = x.shape[0]
     xh, xl = split(x)
     wh, wl = split(w)
-    both = mm(jnp.concatenate([xh, xl], axis=0), wh, dims)
+    if dims == NT and w.shape[1] <= 128:
+        both = jnp.concatenate(
+            [jnp.concatenate([xh, xh], axis=1), jnp.concatenate([xl, xl], axis=1)], axis=0
+        )
+        both = mm(both, jnp.concatenate([wh, wl], axis=1), dims)
+        return both[:m] + both[m:]
+    both = jnp.concatenate([xh, xl], axis=0)
+    if dims == NN and w.shape[1] % 128 == 0:
+        n = w.shape[1]
+        both = mm(both, jnp.concatenate([wh, wl], axis=1), dims)
+        return both[:m, :n] + both[m:, :n] + both[:m, n:]
+    both = mm(both, wh, dims)
     return both[:m] + both[m:] + mm(xh, wl, dims)
+
+
+def dot2(x, w, dims=NN):
+    m = x.shape[0]
+    xh, xl = split(x)
+    both = mm(jnp.concatenate([xh, xl], axis=0), w, dims)
+    return both[:m] + both[m:]
 
 
 def iota(shape, axis):
@@ -76,7 +95,7 @@
     return jnp.where((column == target) & (lane % 8 == r % 8), 1.0, 0.0).astype(BF16)
 
 
-def assemble(sources, few, lcols, ucols, active, stack, panel, sems):
+def assemble(sources, few, lcols, ucols, active, stack, panel, sems, hots, raw, fence):
     width = U * U // CHUNKS
     copies = {}
     for copy in few:
@@ -101,83 +120,111 @@
     tiles = 16 // CHUNKS
     for copy in few:
         copy.wait()
+
     for half in range(2):
-        hot = one_hot(lcols, ucols, active, half)
-        for t in range(16):
-            if t % tiles == 0:
-                for copy in copies[half, t // tiles]:
-                    copy.wait()
-            rows = stack[half, :, :, pl.ds(256 * t, 256)].reshape(256, 256)
-            tile = mm(hot, rows, NN)
-            for s in range(2):
-                even = tile[0:72, 128 * s : 128 * s + 128]
-                odd = tile[72:144, 128 * s : 128 * s + 128]
-                i = 4 * t + 2 * s
-                first = jnp.where(low, even, swap_halves(odd))
-                second = jnp.where(low, swap_halves(even), odd)
-                for c2 in range(9):
-                    base = (c2 * 16 + 8 * half) * PITCH + i
-                    panel[pl.ds(base, 8, stride=PITCH), :] = first[8 * c2 : 8 * c2 + 8]
-                    panel[pl.ds(base + 1, 8, stride=PITCH), :] = second[8 * c2 : 8 * c2 + 8]
+        hots[half] = one_hot(lcols, ucols, active, half)
+    pieces = [(half, first) for half in range(2) for first in range(0, 16, PIECE)]
+    for n in range(len(pieces) + 1):
+        if n < len(pieces) and pieces[n][1] % tiles == 0:
+            for copy in copies[pieces[n][0], pieces[n][1] // tiles]:
+                copy.wait()
+
+        @fence
+        def _():
+            if n < len(pieces):
+                half, first = pieces[n]
+                for t in range(PIECE):
+                    lanes = pl.ds(256 * (first + t), 256)
+                    raw[n % 2, t] = mm(hots[half], stack[half, :, :, lanes].reshape(256, 256), NN)
+            if n:
+                half, first = pieces[n - 1]
+                for t in range(PIECE):
+                    for s in range(2):
+                        even = raw[(n - 1) % 2, t, 0:72, pl.ds(128 * s, 128)]
+                        odd = raw[(n - 1) % 2, t, 72:144, pl.ds(128 * s, 128)]
+                        i = 4 * (first + t) + 2 * s
+                        panel[half][pl.ds(i, 72, stride=PITCH), :] = jnp.where(low, even, swap_halves(odd))
+                        panel[half][pl.ds(i + 1, 72, stride=PITCH), :] = jnp.where(low, swap_halves(even), odd)
 
 
 def block(panel, c2, k):
-    return panel[pl.ds((c2 * 16 + k) * PITCH, U), :]
+    return panel[k // 8][pl.ds((c2 * 8 + k % 8) * PITCH, U), :]
 
 
 def column_blocks(panel, c2, first, last):
     return jnp.concatenate([block(panel, c2, k) for k in range(first, last)], axis=0)
 
 
-def pair_operator(panel, c):
+def group_blocks(panel, s, first, last):
+    return jnp.concatenate([column_blocks(panel, 2 * s + d, first, last) for d in range(2)], axis=1)
+
+
+def operators(panel, ops, fops):
     low = lower_half()
-    zeros = jnp.zeros((U, 128), F32)
-    even, odd = block(panel, c, 2 * c), block(panel, c, 2 * c + 1)
-    right = jnp.where(low, 0.0, odd)
-    inner = dot3(jnp.where(low, even, 0.0), jnp.concatenate([jnp.where(low, 0.0, even), zeros], axis=0))
-    inner = dot3(inner, jnp.concatenate([zeros, right], axis=0))
-    return jnp.concatenate([jnp.where(low, even, -inner), right], axis=0)
-
-
-def forward(rhs, active, panel, work, gt, hacc, ops):
-    live = (iota((1, NB * U), 1) // U) < active
+    zeros = jnp.zeros((128, 128), F32)
+    eye = jnp.where(iota((128, 128), 0) == iota((128, 128), 1), 1.0, 0.0)
+    evens = [block(panel, c, 2 * c) for c in range(8)]
+    odds = [block(panel, c, 2 * c + 1) for c in range(8)]
+    fs = [eye - jnp.concatenate([zeros[:U], jnp.where(low, odd, 0.0)], axis=0) for odd in odds]
+    lowers = [dot3(fs[2 * s + 1], column_blocks(panel, 2 * s, 4 * s + 2, 4 * s + 4)) for s in range(4)]
+    inners = [dot3(even[:, :U], jnp.where(low, 0.0, even)) for even in evens]
+    rights = [jnp.where(low, 0.0, odd) for odd in odds]
+    inners = [swap_halves(inner)[:, :U] for inner in inners]
+    inners = [dot2(inner, right.astype(BF16)) for inner, right in zip(inners, rights)]
+    lowers = [dot3(lowers[s], fs[2 * s]) for s in range(4)]
+    bs = [
+        jnp.concatenate([jnp.where(low, even, -inner), right], axis=0)
+        for even, inner, right in zip(evens, inners, rights)
+    ]
+    uppers = [dot3(bs[2 * s], column_blocks(panel, 2 * s + 1, 4 * s, 4 * s + 2)) for s in range(4)]
+    for s in range(4):
+        fops[s, 0:128, 0:128] = fs[2 * s]
+        fops[s, 0:128, 128:256] = zeros
+        fops[s, 128:256, 0:128] = -lowers[s]
+        fops[s, 128:256, 128:256] = fs[2 * s + 1]
+    uppers = [dot3(uppers[s], bs[2 * s + 1]) for s in range(4)]
+    for s in range(4):
+        ops[s, 0:128, 0:128] = bs[2 * s]
+        ops[s, 0:128, 128:256] = -uppers[s]
+        ops[s, 128:256, 0:128] = zeros
+        ops[s, 128:256, 128:256] = bs[2 * s + 1]
+
+
+def forward(rhs, active, panel, work, gt, hacc, ops, fops):
     low = lower_half()
     eye = (iota((128, 128), 0) == iota((128, 128), 1)).astype(BF16)
-    seeds = -mm(eye, column_blocks(panel, 8, 0, NB).astype(BF16), NT)
+    last = jnp.zeros((N1, 128), F32)
+    hacc[...] = jnp.where(iota((U, NB * U), 0) == iota((U, NB * U), 1), 1.0, 0.0)
+    live = (iota((1, NB * U), 1) // U) < active
     work[0:R, :] = jnp.where(live, rhs[...], 0.0)
-    work[R:, :] = seeds
-    for c in range(8):
-        ops[pl.ds(128 * c, 128), :] = pair_operator(panel, c)
-    hacc[...] = jnp.where(iota((U, NB * U), 0) == iota((U, NB * U), 1), 1.0, 0.0)
-    zeros = jnp.zeros((U, 128), F32)
-    last = jnp.zeros((N1, 128), F32)
-    for c in range(8):
-        here = pl.ds(128 * c, 128)
-        w = work[0:N1, here]
-        inner = jnp.concatenate([zeros, jnp.where(low, block(panel, c, 2 * c + 1), 0.0)], axis=0)
-        x = w - dot3(w, inner, NT)
+    work[R:, :] = -mm(eye, column_blocks(panel, 8, 0, NB).astype(BF16), NT)
+    operators(panel, ops, fops)
+    for s in range(4):
+        here = pl.ds(256 * s, 256)
+        x = dot3(work[0:N1, here], fops[s], NT)
+        g = dot3(hacc[:, here], ops[s])
+        if s < 3:
+            rest = pl.ds(256 * (s + 1), 256 * (3 - s))
+            work[0:N1, rest] -= dot3(x, group_blocks(panel, s, 4 * s + 4, NB), NT)
+            weights = [group_blocks(panel, d, 4 * s, 4 * s + 4) for d in range(s + 1, 4)]
+            hacc[:, rest] -= dot3(g, jnp.concatenate(weights, axis=1))
         work[0:N1, here] = x
-        g = dot3(hacc[:, here], ops[here, :])
         gt[:, here] = g
-        mine = 2 * c + jnp.where(low, 0, 1) == active - 1
-        last = last + jnp.where(mine, x, 0.0)
-        if c < 7:
-            rest = pl.ds(128 * (c + 1), 128 * (7 - c))
-            work[0:N1, rest] -= dot3(x, column_blocks(panel, c, 2 * c + 2, NB), NT)
-            weights = [column_blocks(panel, d, 2 * c, 2 * c + 2) for d in range(c + 1, 8)]
-            hacc[:, rest] -= dot3(g, jnp.concatenate(weights, axis=1))
+        for d in range(2):
+            mine = 4 * s + 2 * d + jnp.where(low, 0, 1) == active - 1
+            last = last + jnp.where(mine, x[:, 128 * d : 128 * d + 128], 0.0)
     boundary = last + swap_halves(last)
     weights = jnp.concatenate([jnp.zeros((U, NB * U), F32), gt[...]], axis=0)
     z0 = dot3(work[...], weights, NT)
     return jnp.concatenate([jnp.where(low, boundary, z0[:N1]), z0[N1:]], axis=0)
 
 
-def backward_step(c, panel, work, zbuf, ops):
-    here = pl.ds(128 * c, 128)
-    z = dot3(work[:, here], ops[here, :], NT)
+def backward_step(s, panel, work, zbuf, ops):
+    here = pl.ds(256 * s, 256)
+    z = dot3(work[:, here], ops[s], NT)
     zbuf[:, here] = z
-    if c:
-        work[:, pl.ds(0, 128 * c)] -= dot3(z, column_blocks(panel, c, 0, 2 * c), NT)
+    if s:
+        work[:, pl.ds(0, 256 * s)] -= dot3(z, group_blocks(panel, s, 0, 4 * s), NT)
 
 
 def unpack(m):
@@ -217,19 +264,21 @@
     levels, rhs_in, lower, upper, diag, llow, lup, lcols_in, ucols_in, counts, *rest
 ):
     if levels is None:
-        maps, zout, stack, panel, work, zbuf, gt, hacc, ops, in_sems, rhs, lcols, ucols, few_sems = rest
+        maps, zout, stack, panel0, panel1, work, zbuf, gt, hacc, ops, fops, in_sems, rhs, lcols, ucols, few_sems, hots, raw = rest
         few = [
             pltpu.make_async_copy(src, dst, few_sems.at[n])
             for n, (src, dst) in enumerate(((lcols_in, lcols), (ucols_in, ucols), (rhs_in, rhs)))
         ]
         active = counts[0]
-        assemble((lower, upper, diag, llow, lup), few, lcols, ucols, active, stack, panel, in_sems)
-        maps[...] = pack(forward(rhs, active, panel, work, gt, hacc, ops))
-        for c in reversed(range(8)):
-            backward_step(c, panel, work, zout, ops)
+        panel = (panel0, panel1)
+        fence = lambda f: f()
+        assemble((lower, upper, diag, llow, lup), few, lcols, ucols, active, stack, panel, in_sems, hots, raw, fence)
+        maps[...] = pack(forward(rhs, active, panel, work, gt, hacc, ops, fops))
+        for s in reversed(range(4)):
+            backward_step(s, panel, work, zout, ops)
         return
     (
-        out, stack, panel, work, zbuf, gt, hacc, ops, in_sems, rhs, lcols, ucols, few_sems,
+        out, stack, panel0, panel1, work, zbuf, gt, hacc, ops, fops, in_sems, rhs, lcols, ucols, few_sems, hots, raw,
         b_core, b_y, b_z, b_x, y_pairs, z_pairs, z_quads, sides,
         s_core, r_core, s_y, r_y, s_fy, r_fy, s_z, r_z, s_fz, r_fz, s_x, r_x, s_fx, r_fx,
     ) = rest
@@ -291,14 +340,15 @@
         for handover in copies[1]:
             handover.wait()
 
-    fence = pl.when(chain >= 0)
     few = [
         pltpu.make_async_copy(src, dst, few_sems.at[n])
         for n, (src, dst) in enumerate(((lcols_in, lcols), (ucols_in, ucols), (rhs_in, rhs)))
     ]
     active = counts[0]
-    assemble((lower, upper, diag, llow, lup), few, lcols, ucols, active, stack, panel, in_sems)
-    b_core[side] = pack(forward(rhs, active, panel, work, gt, hacc, ops))
+    panel = (panel0, panel1)
+    fence = pl.when(chain + zz < 777)
+    assemble((lower, upper, diag, llow, lup), few, lcols, ucols, active, stack, panel, in_sems, hots, raw, fence)
+    b_core[side] = pack(forward(rhs, active, panel, work, gt, hacc, ops, fops))
     pl.semaphore_wait(barrier, len(peers))
 
     core = remote(b_core.at[side], b_core.at[side], s_core, r_core, at_core())
@@ -313,8 +363,8 @@
 
     @fence
     def _():
-        for c in (7, 6, 5):
-            backward_step(c, panel, work, zbuf, ops)
+        for s in (3, 2):
+            backward_step(s, panel, work, zbuf, ops)
 
     finish(ys)
 
@@ -329,8 +379,8 @@
 
     @fence
     def _():
-        for c in (4, 3, 2, 1, 0):
-            backward_step(c, panel, work, zbuf, ops)
+        for s in (1, 0):
+            backward_step(s, panel, work, zbuf, ops)
 
     @fence
     def _():
@@ -401,17 +451,21 @@
     lower, upper, diag, llow, lup = (pltpu.with_memory_space_constraint(v, pltpu.HBM) for v in (lower, upper, diag, llow, lup))
     scratch = [
         pltpu.VMEM((2, 32, 8, U * U), BF16),
-        pltpu.VMEM((144 * PITCH, 128), F32),
+        pltpu.VMEM((72 * PITCH, 128), F32),
+        pltpu.VMEM((72 * PITCH, 128), F32),
         pltpu.VMEM((N2, cols), F32),
         pltpu.VMEM((N2, cols), F32),
         pltpu.VMEM((U, cols), F32),
         pltpu.VMEM((U, cols), F32),
-        pltpu.VMEM((cols, 128), F32),
+        pltpu.VMEM((4, 256, 256), F32),
+        pltpu.VMEM((4, 256, 256), F32),
         dma((5, 2 * CHUNKS)),
         pltpu.VMEM((R, cols), F32),
         pltpu.VMEM((NB, KL), jnp.int32),
         pltpu.VMEM((NB, KL), jnp.int32),
         dma((3,)),
+        pltpu.VMEM((2, 144, 256), BF16),
+        pltpu.VMEM((2, PIECE, 144, 256), F32),
     ]
     if levels is None:
         outs = (jax.ShapeDtypeStruct((PACKED, 128), F32), jax.ShapeDtypeStruct((N2, cols), F32))

time: 44 us -> 42.5 us (0.966)
  Pallas kernels: 42.7 us -> 41.1 us
    pallas_call x1, Pallas kernels: 42.7 us -> 41.1 us  [local(): pl.pallas_call(functools.partial(kernel, levels), out_shape=outs, in_spec...]
where the time goes in v5:
time: 42.5 us; the launch traced here: 42.4 us
  Pallas kernels  41.1 us (97%)
  between operations  0.66 us (2%)
  local copies, waits for them, and re-layouts  0.62 us (1%)
    pallas_call x1, Pallas kernels, local(): pl.pallas_call(functools.partial(kernel, levels), out_shape=outs, in_spec...  41.1 us

profile of v5, /device:TPU:1, one launch (start us, length us, event | category | flops | bytes accessed | tf_op | source)
XLA Modules:
  0.0 42.4 jit_solution(2786206965618956543)
XLA Ops:
  0.7 41.1 %ilu_apply.1 = f32[8,1024]{1,0:T(8,128)S(1)} custom-call(f32[8,1024]{1,0:T(8,128)} %rhs_in.1, bf16[13,16,4096]{2,1,0:T(8,128)(2,1)} %bitcast.5, bf16[13,16,4096]{2,1,0:T(8,128)(2,1)} %bitcast.6, bf16[1,16,4096]{2,1,0:T(8,128)(2,1)} %bitcast.7, bf16[1,16,4096]{2,1,0:T(8,128)(2,1)} %bitcast.8, bf16[1,16,4096]{2,1,0:T(8,128)(2,1)} %bitcast.9, ...), custom_call_target="tpu_custom_call" | custom-call | tf_op jit(solution)/shard_map/ilu_apply/pallas_call | solution.py:483
  41.8 0.6 %copy.12 = f32[8,1024]{1,0:T(8,128)} copy(f32[8,1024]{1,0:T(8,128)S(1)} %ilu_apply.1) | data formatting | bytes 65536

commit v6 on v5

--- a/solution.py
+++ b/solution.py
@@ -15,7 +15,6 @@
 N2 = R + 2 * U
 PACKED = R + U + U // 2
 PITCH = 72
-HALF = 56
 F32 = jnp.float32
 BF16 = jnp.bfloat16
 MESH = pl.DeviceIdType.MESH
@@ -279,8 +278,8 @@
         return
     (
         out, stack, panel0, panel1, work, zbuf, gt, hacc, ops, fops, in_sems, rhs, lcols, ucols, few_sems, hots, raw,
-        b_core, b_y, b_z, b_x, y_pairs, z_pairs, z_quads, sides,
-        s_core, r_core, s_y, r_y, s_fy, r_fy, s_z, r_z, s_fz, r_fz, s_x, r_x, s_fx, r_fx,
+        b_core, b_y, b_z, b_x, b_half, y_pairs, z_pairs, z_near, sides,
+        s_core, r_core, s_half, r_half, s_sib, r_sib, s_y, r_y, s_z, r_z, s_x, r_x,
     ) = rest
     nx, nz, ny = levels
     chain = lax.axis_index("chain")
@@ -295,15 +294,15 @@
     def at_y(k):
         return (chain - y + (y + k) % ny, side)
 
-    def at_z(k):
-        return (chain - zz * ny + ((zz + k) % nz) * ny, side)
+    def at_z(k, core):
+        return (chain - zz * ny + ((zz + k) % nz) * ny, core)
 
     def at_x(k):
         return (((x + k) % nx) * (ny * nz) + chain % (ny * nz), side)
 
     peers = [at_core()]
     peers += [at_y(k) for k in range(1, ny)]
-    peers += [at_z(k) for k in range(1, nz)]
+    peers += [at_z(k, core) for k in range(1, nz) for core in range(2)]
     peers += [at_x(k) for k in range(1, nx)]
     barrier = pltpu.get_barrier_semaphore()
     for peer in peers:
@@ -314,31 +313,40 @@
             src_ref=src, dst_ref=dst, send_sem=send, recv_sem=recv, device_id=peer, device_id_type=MESH
         )
 
-    mine = pl.ds(pl.multiple_of(side * HALF, 8), HALF)
-
-    def put(buf, index, m):
-        buf[index, 0:PACKED] = pack(m)
-        buf[index, PACKED:] = jnp.zeros((2 * HALF - PACKED, 128), F32)
-
-    def ring(buf, index, count, peer_of, send, recv, send_on, recv_on):
-        arrivals, handovers = [], []
+    def ring(buf, index, count, peer_of, send, recv):
+        copies = []
         for k in sorted(range(1, count), key=lambda k: min(k, count - k)):
-            part = buf.at[index, mine]
-            arrivals.append(remote(part, part, send.at[k - 1], recv.at[k - 1], peer_of(k)))
-            part = buf.at[(index + count - k) % count, mine]
-            handovers.append(remote(part, part, send_on.at[k - 1], recv_on.at[k - 1], at_core()))
-        for copy in arrivals:
+            copies.append(remote(buf.at[index], buf.at[index], send.at[k - 1], recv.at[k - 1], peer_of(k)))
+        for copy in copies:
             copy.start()
-        return arrivals, handovers
+        return copies
 
     def finish(copies):
-        for arriving, handover in zip(*copies):
-            arriving.wait_recv()
-            handover.start()
-        for arriving in copies[0]:
-            arriving.wait_send()
-        for handover in copies[1]:
-            handover.wait()
+        for copy in copies:
+            copy.wait()
+
+    half = nz // 2
+    home = zz // half
+    order = sorted(range(1, nz), key=lambda k: min(k, nz - k))
+
+    def z_copy(k):
+        return remote(b_z.at[zz], b_z.at[zz], s_z.at[k - 1], r_z.at[k - 1], at_z(k, home))
+
+    def z_start():
+        for k in order:
+            @pl.when(side == (0 if k <= half else 1))
+            def _():
+                z_copy(k).start()
+
+    def z_finish():
+        for k in order:
+            @pl.when(((zz + nz - k) % nz) // half == side)
+            def _():
+                z_copy(k).wait_recv()
+        for k in order:
+            @pl.when(side == (0 if k <= half else 1))
+            def _():
+                z_copy(k).wait_send()
 
     few = [
         pltpu.make_async_copy(src, dst, few_sems.at[n])
@@ -357,9 +365,9 @@
 
     @fence
     def _():
-        put(b_y, y, compose(unpack(b_core[0]), unpack(b_core[1])))
-
-    ys = ring(b_y, y, ny, at_y, s_y, r_y, s_fy, r_fy)
+        b_y[y] = pack(compose(unpack(b_core[0]), unpack(b_core[1])))
+
+    ys = ring(b_y, y, ny, at_y, s_y, r_y)
 
     @fence
     def _():
@@ -370,12 +378,12 @@
 
     @fence
     def _():
-        nodes = [compose(unpack(b_y[i, 0:PACKED]), unpack(b_y[i + 1, 0:PACKED])) for i in range(0, ny, 2)]
+        nodes = [compose(unpack(b_y[i]), unpack(b_y[i + 1])) for i in range(0, ny, 2)]
         for i, node in enumerate(nodes):
             y_pairs[i] = node
-        put(b_z, zz, compose(*nodes))
-
-    zs = ring(b_z, zz, nz, at_z, s_z, r_z, s_fz, r_fz)
+        b_z[zz] = pack(compose(*nodes))
+
+    z_start()
 
     @fence
     def _():
@@ -386,32 +394,57 @@
     def _():
         before = after = identity_map()
         before, after = narrow(side == 1, unpack(b_core[1 - side]), before, after)
-        before, after = narrow(y % 2 == 1, unpack(b_y[y + 1 - 2 * (y % 2), 0:PACKED]), before, after)
+        before, after = narrow(y % 2 == 1, unpack(b_y[y + 1 - 2 * (y % 2)]), before, after)
         before, after = narrow(y // 2 == 1, y_pairs[1 - y // 2], before, after)
         sides[0] = before
         sides[1] = after
 
-    finish(zs)
-
-    @fence
-    def _():
-        nodes = [compose(unpack(b_z[i, 0:PACKED]), unpack(b_z[i + 1, 0:PACKED])) for i in range(0, nz, 2)]
+    z_finish()
+    first = side * half
+    sibling = zz + 1 - 2 * (zz % 2)
+
+    @fence
+    def _():
+        nodes = [compose(unpack(b_z[first + i]), unpack(b_z[first + i + 1])) for i in range(0, half, 2)]
         for i, node in enumerate(nodes):
             z_pairs[i] = node
-        nodes = [compose(nodes[i], nodes[i + 1]) for i in range(0, nz // 2, 2)]
-        for i, node in enumerate(nodes):
-            z_quads[i] = node
-        put(b_x, x, compose(*nodes))
-
-    xs = ring(b_x, x, nx, at_x, s_x, r_x, s_fx, r_fx)
+        b_half[side] = pack(compose(*nodes))
+
+    swap = remote(b_half.at[side], b_half.at[side], s_half, r_half, at_core())
+    swap.start()
+    leaf = remote(b_z.at[sibling], b_z.at[sibling], s_sib.at[0], r_sib.at[0], at_core())
+    near = remote(z_near, z_near, s_sib.at[1], r_sib.at[1], at_core())
+
+    @pl.when(home == side)
+    def _():
+        z_near[...] = z_pairs[1 - (zz % half) // 2]
+        leaf.start()
+        near.start()
+
+    swap.wait()
+
+    @fence
+    def _():
+        b_x[x] = pack(compose(unpack(b_half[0]), unpack(b_half[1])))
+
+    xs = ring(b_x, x, nx, at_x, s_x, r_x)
+
+    @pl.when(home == side)
+    def _():
+        leaf.wait_send()
+        near.wait_send()
+
+    @pl.when(home != side)
+    def _():
+        leaf.wait_recv()
+        near.wait_recv()
 
     @fence
     def _():
         before, after = sides[0], sides[1]
-        before, after = narrow(zz % 2 == 1, unpack(b_z[zz + 1 - 2 * (zz % 2), 0:PACKED]), before, after)
-        pair = zz // 2
-        before, after = narrow(pair % 2 == 1, z_pairs[pair + 1 - 2 * (pair % 2)], before, after)
-        before, after = narrow(zz // 4 == 1, z_quads[1 - zz // 4], before, after)
+        before, after = narrow(zz % 2 == 1, unpack(b_z[sibling]), before, after)
+        before, after = narrow((zz % half) // 2 == 1, z_near[...], before, after)
+        before, after = narrow(home == 1, unpack(b_half[1 - home]), before, after)
         sides[0] = before
         sides[1] = after
 
@@ -429,7 +462,7 @@
     for j in reversed(range(nx - 1)):
         q = jnp.where(x == j, q_run, q)
         if j:
-            q_run = dot3(q_run, unpack(b_x[j, 0:PACKED])[N1:, U:]) + ends[j][:, U:]
+            q_run = dot3(q_run, unpack(b_x[j])[N1:, U:]) + ends[j][:, U:]
     own = unpack(b_core[side])
     before, after = sides[0], sides[1]
     p = dot3(p, before[R:N1, :U]) + before[:R, :U]
@@ -473,10 +506,9 @@
     else:
         nx, nz, ny = levels
         outs = jax.ShapeDtypeStruct((R, cols), F32)
-        scratch += [pltpu.VMEM((2, PACKED, 128), F32)]
-        scratch += [pltpu.VMEM((n, 2 * HALF, 128), F32) for n in (ny, nz, nx)]
-        scratch += [pltpu.VMEM((n, N2, 128), F32) for n in (ny // 2, nz // 2, nz // 4, 2)]
-        scratch += [dma, dma] + [dma((n - 1,)) for n in (ny, nz, nx) for _ in range(4)]
+        scratch += [pltpu.VMEM((n, PACKED, 128), F32) for n in (2, ny, nz, nx, 2)]
+        scratch += [pltpu.VMEM(m + (N2, 128), F32) for m in ((ny // 2,), (nz // 4,), (), (2,))]
+        scratch += [dma] * 4 + [dma((2,))] * 2 + [dma((n - 1,)) for n in (ny, ny, nz, nz, nx, nx)]
         params = pltpu.CompilerParams(
             collective_id=0, has_side_effects=True, vmem_limit_bytes=48000000
         )

time: 42.5 us -> 41.4 us (0.974)
  Pallas kernels: 41.1 us -> 40 us
    pallas_call x1, Pallas kernels: 41.1 us -> 40 us  [local(): pl.pallas_call(functools.partial(kernel, levels), out_shape=outs, in_spec...]
where the time goes in v6:
time: 41.4 us; the launch traced here: 41.3 us
  Pallas kernels  40 us (97%)
  between operations  0.66 us (2%)
  local copies, waits for them, and re-layouts  0.62 us (1%)
    pallas_call x1, Pallas kernels, local(): pl.pallas_call(functools.partial(kernel, levels), out_shape=outs, in_spec...  40 us

profile of v6, /device:TPU:1, one launch (start us, length us, event | category | flops | bytes accessed | tf_op | source)
XLA Modules:
  0.0 41.3 jit_solution(8965169734542657040)
XLA Ops:
  0.7 40.0 %ilu_apply.1 = f32[8,1024]{1,0:T(8,128)S(1)} custom-call(f32[8,1024]{1,0:T(8,128)} %rhs_in.1, bf16[13,16,4096]{2,1,0:T(8,128)(2,1)} %bitcast.5, bf16[13,16,4096]{2,1,0:T(8,128)(2,1)} %bitcast.6, bf16[1,16,4096]{2,1,0:T(8,128)(2,1)} %bitcast.7, bf16[1,16,4096]{2,1,0:T(8,128)(2,1)} %bitcast.8, bf16[1,16,4096]{2,1,0:T(8,128)(2,1)} %bitcast.9, ...), custom_call_target="tpu_custom_call" | custom-call | tf_op jit(solution)/shard_map/ilu_apply/pallas_call | solution.py:515
  40.6 0.6 %copy.12 = f32[8,1024]{1,0:T(8,128)} copy(f32[8,1024]{1,0:T(8,128)S(1)} %ilu_apply.1) | data formatting | bytes 65536

commit v7 on v6

--- a/solution.py
+++ b/solution.py
@@ -315,7 +315,7 @@
 
     def ring(buf, index, count, peer_of, send, recv):
         copies = []
-        for k in sorted(range(1, count), key=lambda k: min(k, count - k)):
+        for k in sorted(range(1, count), key=lambda k: -min(k, count - k)):
             copies.append(remote(buf.at[index], buf.at[index], send.at[k - 1], recv.at[k - 1], peer_of(k)))
         for copy in copies:
             copy.start()
@@ -327,7 +327,7 @@
 
     half = nz // 2
     home = zz // half
-    order = sorted(range(1, nz), key=lambda k: min(k, nz - k))
+    order = sorted(range(1, nz), key=lambda k: -min(k, nz - k))
 
     def z_copy(k):
         return remote(b_z.at[zz], b_z.at[zz], s_z.at[k - 1], r_z.at[k - 1], at_z(k, home))

time: 41.4 us -> 39.7 us (0.959)
  Pallas kernels: 40 us -> 38.3 us
    pallas_call x1, Pallas kernels: 40 us -> 38.3 us  [local(): pl.pallas_call(functools.partial(kernel, levels), out_shape=outs, in_spec...]
where the time goes in v7:
time: 39.7 us; the launch traced here: 39.6 us
  Pallas kernels  38.3 us (96%)
  between operations  0.66 us (2%)
  local copies, waits for them, and re-layouts  0.62 us (2%)
    pallas_call x1, Pallas kernels, local(): pl.pallas_call(functools.partial(kernel, levels), out_shape=outs, in_spec...  38.3 us

profile of v7, /device:TPU:1, one launch (start us, length us, event | category | flops | bytes accessed | tf_op | source)
XLA Modules:
  0.0 39.6 jit_solution(9310134100358115720)
XLA Ops:
  0.7 38.3 %ilu_apply.1 = f32[8,1024]{1,0:T(8,128)S(1)} custom-call(f32[8,1024]{1,0:T(8,128)} %rhs_in.1, bf16[13,16,4096]{2,1,0:T(8,128)(2,1)} %bitcast.5, bf16[13,16,4096]{2,1,0:T(8,128)(2,1)} %bitcast.6, bf16[1,16,4096]{2,1,0:T(8,128)(2,1)} %bitcast.7, bf16[1,16,4096]{2,1,0:T(8,128)(2,1)} %bitcast.8, bf16[1,16,4096]{2,1,0:T(8,128)(2,1)} %bitcast.9, ...), custom_call_target="tpu_custom_call" | custom-call | tf_op jit(solution)/shard_map/ilu_apply/pallas_call | solution.py:515
  39.0 0.6 %copy.12 = f32[8,1024]{1,0:T(8,128)} copy(f32[8,1024]{1,0:T(8,128)S(1)} %ilu_apply.1) | data formatting | bytes 65536

commit v8 on v7

--- a/solution.py
+++ b/solution.py
@@ -313,17 +313,39 @@
             src_ref=src, dst_ref=dst, send_sem=send, recv_sem=recv, device_id=peer, device_id_type=MESH
         )
 
-    def ring(buf, index, count, peer_of, send, recv):
-        copies = []
-        for k in sorted(range(1, count), key=lambda k: -min(k, count - k)):
-            copies.append(remote(buf.at[index], buf.at[index], send.at[k - 1], recv.at[k - 1], peer_of(k)))
-        for copy in copies:
-            copy.start()
-        return copies
+    def ring(buf, index, peer_of, send, recv):
+        def copy(slot, k, hop):
+            part = buf.at[slot % 4]
+            return remote(part, part, send.at[k - 1], recv.at[k - 1], peer_of(hop))
+
+        far, ahead, behind = (copy(index, k, k) for k in (2, 1, 3))
+
+        @pl.when(side == 0)
+        def _():
+            far.start()
+
+        behind.start()
+        ahead.start()
+        return far, ahead, behind, copy(index + 1, 2, 3)
 
     def finish(copies):
-        for copy in copies:
-            copy.wait()
+        far, ahead, behind, onward = copies
+        behind.wait_recv()
+
+        @pl.when(side == 1)
+        def _():
+            onward.start()
+
+        behind.wait_send()
+        ahead.wait()
+
+        @pl.when(side == 0)
+        def _():
+            far.wait()
+
+        @pl.when(side == 1)
+        def _():
+            onward.wait()
 
     half = nz // 2
     home = zz // half
@@ -367,7 +389,7 @@
     def _():
         b_y[y] = pack(compose(unpack(b_core[0]), unpack(b_core[1])))
 
-    ys = ring(b_y, y, ny, at_y, s_y, r_y)
+    ys = ring(b_y, y, at_y, s_y, r_y)
 
     @fence
     def _():
@@ -427,7 +449,7 @@
     def _():
         b_x[x] = pack(compose(unpack(b_half[0]), unpack(b_half[1])))
 
-    xs = ring(b_x, x, nx, at_x, s_x, r_x)
+    xs = ring(b_x, x, at_x, s_x, r_x)
 
     @pl.when(home == side)
     def _():

time: 39.7 us -> 39.3 us (0.990)
  no operation moved by 1% of the time
where the time goes in v8:
time: 39.3 us; the launch traced here: 39.2 us
  Pallas kernels  38 us (97%)
  between operations  0.66 us (2%)
  local copies, waits for them, and re-layouts  0.62 us (2%)
    pallas_call x1, Pallas kernels, local(): pl.pallas_call(functools.partial(kernel, levels), out_shape=outs, in_spec...  38 us

profile of v8, /device:TPU:1, one launch (start us, length us, event | category | flops | bytes accessed | tf_op | source)
XLA Modules:
  0.0 39.2 jit_solution(6105960151639905907)
XLA Ops:
  0.7 38.0 %ilu_apply.1 = f32[8,1024]{1,0:T(8,128)S(1)} custom-call(f32[8,1024]{1,0:T(8,128)} %rhs_in.1, bf16[13,16,4096]{2,1,0:T(8,128)(2,1)} %bitcast.5, bf16[13,16,4096]{2,1,0:T(8,128)(2,1)} %bitcast.6, bf16[1,16,4096]{2,1,0:T(8,128)(2,1)} %bitcast.7, bf16[1,16,4096]{2,1,0:T(8,128)(2,1)} %bitcast.8, bf16[1,16,4096]{2,1,0:T(8,128)(2,1)} %bitcast.9, ...), custom_call_target="tpu_custom_call" | custom-call | tf_op jit(solution)/shard_map/ilu_apply/pallas_call | solution.py:537
  38.6 0.6 %copy.12 = f32[8,1024]{1,0:T(8,128)} copy(f32[8,1024]{1,0:T(8,128)S(1)} %ilu_apply.1) | data formatting | bytes 65536
